TPU v7x, 512 devices: a whole 4x4x16 slice. The times are simulated.
512 devices in a mesh: space: 64 (over y, z), mode: 8 (over x, core).
Axes of the slice: x: 4, y: 4, z: 16, core: 2. Of those that a mesh axis runs over, the one named last changes fastest.
Arguments:
- guess: float32 [120, 128, 8, 128], P('mode', 'space'), may hold values from -6 to 6
- source: float32 [120, 128, 8, 128], P('mode', 'space'), may hold values from -6 to 6
- mean_coef: float32 [128, 8, 128], P('space'), may hold values from 1 to 4
- fluct_coef: float32 [7, 128, 8, 128], P(None, 'space'), may hold values from -2 to 2
- triples: int32 [3, 1680], replicated, may hold values from 0 to 119, as said below
- coupling: float32 [1680], replicated, may hold values from -1.5 to 1.5
Outputs:
- solution: float32 [120, 128, 8, 128], P('mode', 'space')
- update: float32 [120, 128, 8, 128], P('mode', 'space')
Inputs may be any that keep to these rules, and one draw needn't show every extreme that they name: `triples`: row 0 holds the output mode i, row 1 the coupled mode j, row 2 the term k, which is 1 to 7; every pair (i, k) stands in exactly 2 entries, in no particular order; j is any mode.
All inputs are finite; a program needn't handle non-finite values.
Results may differ from a plain program's by a relative error of at most 0.00019.
Values sent between devices are 32-bit elements; how exact they have to be, the bound alone decides.
No kernel may reach another device: no remote copies, remote signals or barrier semaphores. Data moves between devices by JAX's collectives and lax.ppermute only.
A program may use at most 64 MiB of HBM per device.

v0:
```python
import jax
import jax.numpy as jnp
from jax import lax
from jax.sharding import PartitionSpec as P

ITERS = 3


def extended(cells, sides, width):
    for axis, dim in sides:
        count = lax.axis_size(axis)
        ends = count - 1
        head = lax.slice_in_dim(cells, 0, width, axis=dim)
        tail = lax.slice_in_dim(cells, cells.shape[dim] - width, cells.shape[dim], axis=dim)
        cells = jnp.concatenate(
            [
                lax.ppermute(tail, axis, [(i, (i + 1) % count) for i in range(ends)]),
                cells,
                lax.ppermute(head, axis, [((i + 1) % count, i) for i in range(ends)]),
            ],
            axis=dim,
        )
    return cells


def neighbours(padded):
    centre = padded[..., 1:-1, 1:-1, 1:-1]
    others = [
        padded[..., 2:, 1:-1, 1:-1],
        padded[..., :-2, 1:-1, 1:-1],
        padded[..., 1:-1, 2:, 1:-1],
        padded[..., 1:-1, :-2, 1:-1],
        padded[..., 1:-1, 1:-1, 2:],
        padded[..., 1:-1, 1:-1, :-2],
    ]
    return (centre, others)


def face_terms(padded_coef):
    centre, others = neighbours(padded_coef)
    return [0.5 * (centre + other) for other in others]


def pad_sides(field):
    return jnp.pad(field, ((0, 0), (0, 0), (1, 1), (1, 1)))


def stencil(padded_field, faces):
    centre, others = neighbours(padded_field)
    total = jnp.zeros((centre.shape[0],) + centre.shape[2:], jnp.float32)
    for face, other in zip(faces, others):
        total = total + jnp.sum(face * (centre - other), axis=1)
    return total


def build_table(owned, triples, coupling, modes, terms):
    pick_rows = jnp.where(triples[0][None, :] == owned[:, None], coupling[None, :], 0.0)
    flat_cols = triples[2] * modes + triples[1]
    pick_cols = (flat_cols[:, None] == lax.iota(jnp.int32, terms * modes)[None, :]).astype(
        jnp.float32
    )
    count = owned.shape[0]
    table = jnp.dot(pick_rows, pick_cols, precision=lax.Precision.HIGHEST).reshape(
        count, terms, modes
    )
    identity = (owned[:, None] == lax.iota(jnp.int32, modes)[None, :]).astype(jnp.float32)
    table = jnp.concatenate([table[:, :1, :] + identity[:, None, :], table[:, 1:, :]], axis=1)
    return table.reshape(count * terms, modes)


def diagonal_of(faces):
    diagonal = faces[0][0]
    for face in faces[1:]:
        diagonal = diagonal + face[0]
    return diagonal


def per_device(guess, source, mean_coef, fluct_coef, triples, coupling):
    blocks, planes, rows_y, rows_z = guess.shape
    modes = blocks * lax.axis_size("mode")
    terms = fluct_coef.shape[0] + 1
    coefs = jnp.concatenate([mean_coef[None], fluct_coef], axis=0)
    coef_pad = pad_sides(extended(coefs, (("space", 1),), 1))
    faces = face_terms(coef_pad)
    diagonal = diagonal_of(faces)
    owned = lax.axis_index("mode") * blocks + lax.iota(jnp.int32, blocks)
    mixing = build_table(owned, triples, coupling, modes, terms)
    solution = guess
    update = guess
    for step in range(ITERS):
        piece = lax.all_gather(solution, "mode", axis=0, tiled=True)
        mixed = jnp.dot(mixing, piece.reshape(piece.shape[0], -1), precision=lax.Precision.HIGHEST)
        mixed = mixed.reshape(blocks * terms, planes, rows_y, rows_z)
        mixed = extended(mixed, (("space", 1),), 1)
        padded = pad_sides(mixed).reshape(blocks, terms, planes + 2, rows_y + 2, rows_z + 2)
        image = stencil(padded, faces)
        update = (source - image) / diagonal
        solution = solution + 0.5 * update
    return (solution, update)


def solution(mesh):
    in_specs = (
        P("mode", "space", None, None),
        P("mode", "space", None, None),
        P("space", None, None),
        P(None, "space", None, None),
        P(),
        P(),
    )
    out_specs = (P("mode", "space", None, None), P("mode", "space", None, None))
    return jax.shard_map(
        per_device, mesh=mesh, in_specs=in_specs, out_specs=out_specs, check_vma=False
    )
```

profile of v0, /device:TPU:24, one launch (start us, length us, event | category | flops | bytes accessed | tf_op | source)
XLA Modules:
  0.0 138.6 jit_solution(13225182544695413680)
XLA Ops:
  0.6 0.8 fusion.67
  1.4 11.6 %collective-permute-start = (f32[8,1,8,128]{3,2,1,0:T(8,128)S(1)}, f32[8,1,8,128]{3,2,1,0:T(8,128)S(1)}, u32[]{:S(2)}, u32[]{:S(2)}) collective-permute-start(f32[8,1,8,128]{3,2,1,0:T(8,128)S(1)} %get-tuple-element.37), channel_id=1, source_target_pairs={{8,0},{16,8},{24,16},{32,24},{40,32},{48,40},{56,48},{64,56},{72,6... | collective-permute-start | bytes 98312 | tf_op jit(solution)/shard_map/ppermute | solution.py:19
  13.0 1.9 %collective-permute-start.3 = (f32[8,1,8,128]{3,2,1,0:T(8,128)S(1)}, f32[8,1,8,128]{3,2,1,0:T(8,128)S(1)}, u32[]{:S(2)}, u32[]{:S(2)}) collective-permute-start(f32[8,1,8,128]{3,2,1,0:T(8,128)S(1)} %get-tuple-element.38), channel_id=1, source_target_pairs={{0,8},{8,16},{16,24},{24,32},{32,40},{40,48},{48,56},{56,64},{64,7... | collective-permute-start | bytes 98312 | tf_op jit(solution)/shard_map/ppermute | solution.py:17
  14.9 0.9 slice_reduce_fusion
  15.8 3.0 %fusion = f32[15,960]{1,0:T(8,128)S(1)} fusion(s32[1680]{0:T(1024)S(1)} %get-tuple-element.23, f32[1680]{0:T(1024)} %param.11, s32[1680]{0:T(1024)S(1)} %get-tuple-element.22, s32[15]{0:T(128)S(1)} %iota_add_fusion), kind=kOutput, calls=%fused_computation.5 | convolution fusion | flops 291967200 | bytes 77820 | tf_op jit(solution)/shard_map/dot_general | solution.py:63
  19.0 14.2 %all_gather.9 = f32[120,2,8,128]{3,2,1,0:T(8,128)S(1)} all-gather(f32[15,2,8,128]{3,2,1,0:T(8,128)} %param.6), channel_id=1, replica_groups=mesh['space'=64,'mode'=8] {'mode'}, dimensions={0}, use_global_device_ids=true | all-gather | bytes 1105920 | tf_op jit(solution)/shard_map/all_gather | solution.py:91
  33.2 0.3 copy.63
  33.7 1.2 fusion.48
  35.0 1.9 %collective-permute-start.1 = (f32[120,1,8,128]{3,0,2,1:T(8,128)S(1)}, f32[120,1,8,128]{3,0,2,1:T(8,128)S(1)}, u32[]{:S(2)}, u32[]{:S(2)}) collective-permute-start(f32[120,1,8,128]{3,0,2,1:T(8,128)S(1)} %get-tuple-element.30), channel_id=1, source_target_pairs={{0,8},{8,16},{16,24},{24,32},{32,40},{40,48},{48,56},{56,64},{64,7... | collective-permute-start | bytes 1474568 | tf_op jit(solution)/shard_map/ppermute | solution.py:17
  36.9 6.0 %collective-permute-start.2 = (f32[120,1,8,128]{3,0,2,1:T(8,128)S(1)}, f32[120,1,8,128]{3,0,2,1:T(8,128)S(1)}, u32[]{:S(2)}, u32[]{:S(2)}) collective-permute-start(f32[120,1,8,128]{3,0,2,1:T(8,128)S(1)} %get-tuple-element.31), channel_id=1, source_target_pairs={{8,0},{16,8},{24,16},{32,24},{40,32},{48,40},{56,48},{64,56},{72,6... | collective-permute-start | bytes 1474568 | tf_op jit(solution)/shard_map/ppermute | solution.py:19
  43.6 9.2 %collective-permute-done.1 = f32[120,1,8,128]{3,0,2,1:T(8,128)S(1)} collective-permute-done((f32[120,1,8,128]{3,0,2,1:T(8,128)S(1)}, f32[120,1,8,128]{3,0,2,1:T(8,128)S(1)}, u32[]{:S(2)}, u32[]{:S(2)}) %collective-permute-start.1) | collective-permute-done | bytes 491552 | tf_op jit(solution)/shard_map/ppermute | solution.py:17
  52.7 1.2 collective-permute-done.2
  53.9 2.2 %fusion.3 = f32[15,8,4,10,130]{4,1,0,3,2:T(8,128)S(1)} fusion(f32[120,1,8,128]{3,0,2,1:T(8,128)S(1)} %collective-permute-done.2, f32[120,2,8,128]{3,0,2,1:T(8,128)S(1)} %fusion.48, f32[120,1,8,128]{3,0,2,1:T(8,128)S(1)} %collective-permute-done.1), kind=kLoop, calls=%fused_computation.13 | loop fusion | flops 9360000 | bytes 4462080 | tf_op jit(solution)/shard_map/reshape | solution.py:95
  56.1 2.2 %fusion.41 = (f32[15,2,8,128]{3,0,2,1:T(8,128)S(1)}, f32[15,2,8,128]{3,0,2,1:T(8,128)S(1)}, f32[15,2,8,128]{3,0,2,1:T(8,128)S(1)}, f32[15,2,8,128]{3,0,2,1:T(8,1...) fusion(f32[15,8,4,10,130]{4,1,0,3,2:T(8,128)S(1)} %fusion.3, f32[8,2,8,128]{3,0,2,1:T(8,128)S(1)} %copy.25, ...), kind=kLoop, calls=%fused_computation.72 | loop fusion | flops 4239360 | bytes 8011776 | tf_op jit(solution)/shard_map/reduce_sum | solution.py:52
  58.6 13.6 %all_gather.10 = f32[120,2,8,128]{3,2,1,0:T(8,128)S(1)} all-gather(f32[15,2,8,128]{3,2,1,0:T(8,128)S(1)} %copy.32), channel_id=1, replica_groups=mesh['space'=64,'mode'=8] {'mode'}, dimensions={0}, use_global_device_ids=true | all-gather | bytes 1105920 | tf_op jit(solution)/shard_map/all_gather | solution.py:91
  72.6 1.2 fusion.46
  73.9 1.9 %collective-permute-start.4 = (f32[120,1,8,128]{3,0,2,1:T(8,128)S(1)}, f32[120,1,8,128]{3,0,2,1:T(8,128)S(1)}, u32[]{:S(2)}, u32[]{:S(2)}) collective-permute-start(f32[120,1,8,128]{3,0,2,1:T(8,128)S(1)} %get-tuple-element.28), channel_id=1, source_target_pairs={{0,8},{8,16},{16,24},{24,32},{32,40},{40,48},{48,56},{56,64},{64,7... | collective-permute-start | bytes 1474568 | tf_op jit(solution)/shard_map/ppermute | solution.py:17
  75.9 6.7 %collective-permute-start.5 = (f32[120,1,8,128]{3,0,2,1:T(8,128)S(1)}, f32[120,1,8,128]{3,0,2,1:T(8,128)S(1)}, u32[]{:S(2)}, u32[]{:S(2)}) collective-permute-start(f32[120,1,8,128]{3,0,2,1:T(8,128)S(1)} %get-tuple-element.29), channel_id=1, source_target_pairs={{8,0},{16,8},{24,16},{32,24},{40,32},{48,40},{56,48},{64,56},{72,6... | collective-permute-start | bytes 1474568 | tf_op jit(solution)/shard_map/ppermute | solution.py:19
  82.6 9.6 %collective-permute-done.4 = f32[120,1,8,128]{3,0,2,1:T(8,128)S(1)} collective-permute-done((f32[120,1,8,128]{3,0,2,1:T(8,128)S(1)}, f32[120,1,8,128]{3,0,2,1:T(8,128)S(1)}, u32[]{:S(2)}, u32[]{:S(2)}) %collective-permute-start.4) | collective-permute-done | bytes 491552 | tf_op jit(solution)/shard_map/ppermute | solution.py:17
  92.2 1.2 collective-permute-done.5
  93.3 2.2 %fusion.2 = f32[15,8,4,10,130]{4,1,0,3,2:T(8,128)S(1)} fusion(f32[120,1,8,128]{3,0,2,1:T(8,128)S(1)} %collective-permute-done.5, f32[120,2,8,128]{3,0,2,1:T(8,128)S(1)} %fusion.46, f32[120,1,8,128]{3,0,2,1:T(8,128)S(1)} %collective-permute-done.4), kind=kLoop, calls=%fused_computation.10 | loop fusion | flops 9360000 | bytes 4462080 | tf_op jit(solution)/shard_map/reshape | solution.py:95
  95.5 2.2 %fusion.29 = (f32[15,2,8,128]{3,0,2,1:T(8,128)S(1)}, f32[15,2,8,128]{3,0,2,1:T(8,128)S(1)}, f32[15,2,8,128]{3,0,2,1:T(8,128)S(1)}, f32[15,2,8,128]{3,0,2,1:T(8,1...) fusion(f32[15,8,4,10,130]{4,1,0,3,2:T(8,128)S(1)} %fusion.2, f32[8,2,8,128]{3,0,2,1:T(8,128)S(1)} %copy.25, ...), kind=kLoop, calls=%fused_computation.54 | loop fusion | flops 4239360 | bytes 8011776 | tf_op jit(solution)/shard_map/reduce_sum | solution.py:52
  97.9 13.6 %all_gather.11 = f32[120,2,8,128]{3,2,1,0:T(8,128)S(1)} all-gather(f32[15,2,8,128]{3,2,1,0:T(8,128)S(1)} %copy.35), channel_id=1, replica_groups=mesh['space'=64,'mode'=8] {'mode'}, dimensions={0}, use_global_device_ids=true | all-gather | bytes 1105920 | tf_op jit(solution)/shard_map/all_gather | solution.py:91
  112.0 1.2 fusion.44
  113.3 1.9 %collective-permute-start.6 = (f32[120,1,8,128]{3,0,2,1:T(8,128)S(1)}, f32[120,1,8,128]{3,0,2,1:T(8,128)S(1)}, u32[]{:S(2)}, u32[]{:S(2)}) collective-permute-start(f32[120,1,8,128]{3,0,2,1:T(8,128)S(1)} %get-tuple-element.26), channel_id=1, source_target_pairs={{0,8},{8,16},{16,24},{24,32},{32,40},{40,48},{48,56},{56,64},{64,7... | collective-permute-start | bytes 1474568 | tf_op jit(solution)/shard_map/ppermute | solution.py:17
  115.2 6.5 %collective-permute-start.7 = (f32[120,1,8,128]{3,0,2,1:T(8,128)S(1)}, f32[120,1,8,128]{3,0,2,1:T(8,128)S(1)}, u32[]{:S(2)}, u32[]{:S(2)}) collective-permute-start(f32[120,1,8,128]{3,0,2,1:T(8,128)S(1)} %get-tuple-element.27), channel_id=1, source_target_pairs={{8,0},{16,8},{24,16},{32,24},{40,32},{48,40},{56,48},{64,56},{72,6... | collective-permute-start | bytes 1474568 | tf_op jit(solution)/shard_map/ppermute | solution.py:19
  121.7 9.8 %collective-permute-done.6 = f32[120,1,8,128]{3,0,2,1:T(8,128)S(1)} collective-permute-done((f32[120,1,8,128]{3,0,2,1:T(8,128)S(1)}, f32[120,1,8,128]{3,0,2,1:T(8,128)S(1)}, u32[]{:S(2)}, u32[]{:S(2)}) %collective-permute-start.6) | collective-permute-done | bytes 491552 | tf_op jit(solution)/shard_map/ppermute | solution.py:17
  131.5 1.2 collective-permute-done.7
  132.7 2.2 %fusion.1 = f32[15,8,4,10,130]{4,1,0,3,2:T(8,128)S(1)} fusion(f32[120,1,8,128]{3,0,2,1:T(8,128)S(1)} %collective-permute-done.7, f32[120,2,8,128]{3,0,2,1:T(8,128)S(1)} %fusion.44, f32[120,1,8,128]{3,0,2,1:T(8,128)S(1)} %collective-permute-done.6), kind=kLoop, calls=%fused_computation.7 | loop fusion | flops 9360000 | bytes 4462080 | tf_op jit(solution)/shard_map/reshape | solution.py:95
  134.9 2.2 %fusion.17 = (f32[15,2,8,128]{3,0,2,1:T(8,128)S(1)}, f32[15,2,8,128]{3,0,2,1:T(8,128)S(1)}, f32[15,2,8,128]{3,0,2,1:T(8,128)S(1)}, f32[15,2,8,128]{3,0,2,1:T(8,1...) fusion(f32[15,8,4,10,130]{4,1,0,3,2:T(8,128)S(1)} %fusion.1, f32[8,2,8,128]{3,0,2,1:T(8,128)S(1)} %copy.25, ...), kind=kLoop, calls=%fused_computation.36 | loop fusion | flops 4239360 | bytes 8011776 | tf_op jit(solution)/shard_map/reduce_sum | solution.py:52
  137.2 0.7 copy.38
  137.9 0.7 copy.39
  (37 shorter events, 2.5 us)
Async XLA Ops:
  1.4 41.5 %collective-permute-start = (f32[8,1,8,128]{3,2,1,0:T(8,128)S(1)}, f32[8,1,8,128]{3,2,1,0:T(8,128)S(1)}, u32[]{:S(2)}, u32[]{:S(2)}) collective-permute-start(f32[8,1,8,128]{3,2,1,0:T(8,128)S(1)} %get-tuple-element.37), channel_id=1, source_target_pairs={{8,0},{16,8},{24,16},{32,24},{40,32},{48,40},{56,48},{64,56},{72,6... | collective-permute-start | bytes 98312 | tf_op jit(solution)/shard_map/ppermute | solution.py:19
  13.0 30.0 %collective-permute-start.3 = (f32[8,1,8,128]{3,2,1,0:T(8,128)S(1)}, f32[8,1,8,128]{3,2,1,0:T(8,128)S(1)}, u32[]{:S(2)}, u32[]{:S(2)}) collective-permute-start(f32[8,1,8,128]{3,2,1,0:T(8,128)S(1)} %get-tuple-element.38), channel_id=1, source_target_pairs={{0,8},{8,16},{16,24},{24,32},{32,40},{40,48},{48,56},{56,64},{64,7... | collective-permute-start | bytes 98312 | tf_op jit(solution)/shard_map/ppermute | solution.py:17
  18.8 24.1 %copy-start.1 = (f32[7,2,8,128]{3,2,1,0:T(8,128)S(1)}, f32[7,2,8,128]{3,2,1,0:T(8,128)}, u32[]{:S(2)}) copy-start(f32[7,2,8,128]{3,2,1,0:T(8,128)} %param.9) | copy-start | bytes 172036
  18.8 24.2 %copy-start.3 = (f32[2,8,128]{2,1,0:T(8,128)S(1)}, f32[2,8,128]{2,1,0:T(8,128)}, u32[]{:S(2)}) copy-start(f32[2,8,128]{2,1,0:T(8,128)} %param.8) | copy-start | bytes 24580
  35.0 17.8 %collective-permute-start.1 = (f32[120,1,8,128]{3,0,2,1:T(8,128)S(1)}, f32[120,1,8,128]{3,0,2,1:T(8,128)S(1)}, u32[]{:S(2)}, u32[]{:S(2)}) collective-permute-start(f32[120,1,8,128]{3,0,2,1:T(8,128)S(1)} %get-tuple-element.30), channel_id=1, source_target_pairs={{0,8},{8,16},{16,24},{24,32},{32,40},{40,48},{48,56},{56,64},{64,7... | collective-permute-start | bytes 1474568 | tf_op jit(solution)/shard_map/ppermute | solution.py:17
  36.9 17.0 %collective-permute-start.2 = (f32[120,1,8,128]{3,0,2,1:T(8,128)S(1)}, f32[120,1,8,128]{3,0,2,1:T(8,128)S(1)}, u32[]{:S(2)}, u32[]{:S(2)}) collective-permute-start(f32[120,1,8,128]{3,0,2,1:T(8,128)S(1)} %get-tuple-element.31), channel_id=1, source_target_pairs={{8,0},{16,8},{24,16},{32,24},{40,32},{48,40},{56,48},{64,56},{72,6... | collective-permute-start | bytes 1474568 | tf_op jit(solution)/shard_map/ppermute | solution.py:19
  56.1 2.2 %copy-start = (f32[15,2,8,128]{3,2,1,0:T(8,128)S(1)}, f32[15,2,8,128]{3,2,1,0:T(8,128)}, u32[]{:S(2)}) copy-start(f32[15,2,8,128]{3,2,1,0:T(8,128)} %param.7) | copy-start | bytes 368644
  56.1 2.2 %copy-start.2 = (f32[15,2,8,128]{3,2,1,0:T(8,128)S(1)}, f32[15,2,8,128]{3,2,1,0:T(8,128)}, u32[]{:S(2)}) copy-start(f32[15,2,8,128]{3,2,1,0:T(8,128)} %param.6) | copy-start | bytes 368644
  73.9 18.2 %collective-permute-start.4 = (f32[120,1,8,128]{3,0,2,1:T(8,128)S(1)}, f32[120,1,8,128]{3,0,2,1:T(8,128)S(1)}, u32[]{:S(2)}, u32[]{:S(2)}) collective-permute-start(f32[120,1,8,128]{3,0,2,1:T(8,128)S(1)} %get-tuple-element.28), channel_id=1, source_target_pairs={{0,8},{8,16},{16,24},{24,32},{32,40},{40,48},{48,56},{56,64},{64,7... | collective-permute-start | bytes 1474568 | tf_op jit(solution)/shard_map/ppermute | solution.py:17
  75.9 17.5 %collective-permute-start.5 = (f32[120,1,8,128]{3,0,2,1:T(8,128)S(1)}, f32[120,1,8,128]{3,0,2,1:T(8,128)S(1)}, u32[]{:S(2)}, u32[]{:S(2)}) collective-permute-start(f32[120,1,8,128]{3,0,2,1:T(8,128)S(1)} %get-tuple-element.29), channel_id=1, source_target_pairs={{8,0},{16,8},{24,16},{32,24},{40,32},{48,40},{56,48},{64,56},{72,6... | collective-permute-start | bytes 1474568 | tf_op jit(solution)/shard_map/ppermute | solution.py:19
  113.3 18.2 %collective-permute-start.6 = (f32[120,1,8,128]{3,0,2,1:T(8,128)S(1)}, f32[120,1,8,128]{3,0,2,1:T(8,128)S(1)}, u32[]{:S(2)}, u32[]{:S(2)}) collective-permute-start(f32[120,1,8,128]{3,0,2,1:T(8,128)S(1)} %get-tuple-element.26), channel_id=1, source_target_pairs={{0,8},{8,16},{16,24},{24,32},{32,40},{40,48},{48,56},{56,64},{64,7... | collective-permute-start | bytes 1474568 | tf_op jit(solution)/shard_map/ppermute | solution.py:17
  115.2 17.5 %collective-permute-start.7 = (f32[120,1,8,128]{3,0,2,1:T(8,128)S(1)}, f32[120,1,8,128]{3,0,2,1:T(8,128)S(1)}, u32[]{:S(2)}, u32[]{:S(2)}) collective-permute-start(f32[120,1,8,128]{3,0,2,1:T(8,128)S(1)} %get-tuple-element.27), channel_id=1, source_target_pairs={{8,0},{16,8},{24,16},{32,24},{40,32},{48,40},{56,48},{64,56},{72,6... | collective-permute-start | bytes 1474568 | tf_op jit(solution)/shard_map/ppermute | solution.py:19
where the time goes:
time: 139 us
  blocking collectives  41.3 us (30%)
  starting transfers between devices  38.5 us (28%)
  waiting for transfers between devices  32.1 us (23%)
  other arithmetic  15.6 us (11%)
  matrix products  6.64 us (5%)
  local copies, waits for them, and re-layouts  3.37 us (2%)
    all_gather x3, blocking collectives, per_device(): piece = lax.all_gather(solution, 'mode', axis=0, tiled=True)  41.3 us
    ppermute x4, starting transfers between devices, extended(): lax.ppermute(head, axis, [((i + 1) % count, i) for i in range(ends)])  30.8 us
    ppermute x4, waiting for transfers between devices, extended(): lax.ppermute(tail, axis, [(i, (i + 1) % count) for i in range(ends)])  28.6 us
    ppermute x4, starting transfers between devices, extended(): lax.ppermute(tail, axis, [(i, (i + 1) % count) for i in range(ends)])  7.68 us
    reshape x3, other arithmetic, per_device(): pad_sides(mixed).reshape(blocks, terms, planes + 2, rows_y + 2, rows_z + 2)  6.56 us
    reduce_sum x3, other arithmetic, stencil(): total = total + jnp.sum(face * (centre - other), axis=1)  6.53 us
    dot_general x3, matrix products, per_device(): jnp.dot(mixing, piece.reshape(piece.shape[0], -1), precision=lax.Precisio...  3.65 us
    ppermute x4, waiting for transfers between devices, extended(): lax.ppermute(head, axis, [((i + 1) % count, i) for i in range(ends)])  3.54 us
  transfers between devices with their start and end apart: 8, of which 6 were waited for; matrix products, arithmetic and copies ran while one was open for 5% of the time, Pallas kernels for 0%

commit v1 on v0

v1 whole, which is shorter than its diff:
```python
import jax
import jax.numpy as jnp
import numpy as np
from jax import lax
from jax.experimental import pallas as pl
from jax.experimental.pallas import tpu as pltpu
from jax.sharding import PartitionSpec as P

ITERS = 3
PARTS = 8
BLOCK = 15
MODES = 120
TERMS = 8
Y, Z = 8, 128
ZW = 16
TRI = 5
ROWS = 11

GW, FW, MW = 22, 20, 84


def _segments():
    first, second = [], []
    for plane, low, width in ((0, -2, 20), (1, -2, 20), (-1, -1, 18), (2, -1, 18), (-2, 0, 16), (3, 0, 16)):
        first += [(plane, low + t) for t in range(width)]
    for plane, low, high in ((0, -3, 18), (1, -3, 18), (-1, -2, 17), (2, -2, 17), (-2, -1, 16), (3, -1, 16)):
        second += [(plane, low), (plane, high)]
    for plane in (-3, 4):
        second += [(plane, t) for t in range(ZW)]
    return first, second


def _tables():
    first, second = _segments()
    at0 = {cell: lane for lane, cell in enumerate(first)}
    at1 = {cell: lane for lane, cell in enumerate(second)}

    def g_lane(r, plane, z):
        return (MW * r + GW * plane + z + 3) % 128

    def f_lane(r, plane, z):
        return (MW * r + 2 * GW + FW * plane + z + 2) % 128

    def origin(plane):
        if plane in (0, 1):
            return 0, plane
        if plane in (-2, -1):
            return 1, plane + 2
        return 2, plane - 2

    rows = []

    def add(fill):
        row = np.zeros(128, np.int32)
        for lane, value in fill:
            row[lane] = value
        rows.append(row)
        return len(rows) - 1

    name = {}
    name["v0"] = [add([(l, g_lane(r, origin(p)[1], z)) for l, (p, z) in enumerate(first)]) for r in range(3)]
    name["f"] = [add([(l, f_lane(r, origin(p)[1], z)) for l, (p, z) in enumerate(first)]) for r in range(3)]
    inner = [(l, c) for l, c in enumerate(second) if c[0] not in (-3, 4)]
    name["v1"] = [add([(l, g_lane(r, origin(p)[1], z)) for l, (p, z) in inner]) for r in range(3)]
    name["code0"] = add([(l, origin(p)[0]) for l, (p, z) in enumerate(first)])
    name["code1"] = add([(l, {-3: 3, 4: 4}.get(p, origin(p)[0])) for l, (p, z) in enumerate(second)])
    name["near0"], name["near1"], name["which"] = [], [], []
    for dp, dz in ((0, 1), (0, -1), (1, 0), (-1, 0)):
        zero, one, mask = [], [], []
        for l, (p, z) in enumerate(first):
            cell = (p + dp, z + dz)
            if cell in at0:
                zero.append((l, at0[cell]))
            else:
                one.append((l, at1[cell]))
                mask.append((l, 1))
        name["near0"].append(add(zero))
        name["near1"].append(add(one))
        name["which"].append(add(mask))
    own = []
    for l in range(128):
        q = l % 32
        own.append((l, at0[(q // 16, q % 16)]))
    name["own"] = add(own)
    while len(rows) % 8:
        rows.append(np.zeros(128, np.int32))
    return np.stack(rows), name


TABLE, AT = _tables()


def _take(tile, index):
    return jnp.take_along_axis(tile, index, axis=1, mode="promise_in_bounds")


def _lane():
    return lax.broadcasted_iota(jnp.int32, (Y, 128), 1)


def _roll(tile, amount):
    amount %= 128
    return pltpu.roll(tile, amount, 1) if amount else tile


def _send_kernel(which_ref, guess_ref, source_ref, mean_ref, fluct_ref, out_ref):
    lane = _lane()

    def trimmed(tile, d, offset):
        if d == 0:
            tile = jnp.where(offset < 0, 0.0, tile)
        if d == PARTS - 1:
            tile = jnp.where(offset >= ZW, 0.0, tile)
        return tile

    def offsets(lanes):
        q = lanes % MW
        g = q % GW - 3
        f = (q - 2 * GW) % FW - 2
        return jnp.where(q < 2 * GW, g, f)

    low, high = offsets(lane), offsets(lane + 128)

    def triple(t, _):
        m = 3 * t
        a, b, c = ([(guess_ref[m + r, p], source_ref[m + r, p]) for p in range(2)] for r in range(3))
        for d in range(PARTS):
            base = -ZW * d
            parts = [
                (0, a[0][0], 3), (22, a[1][0], 25), (44, a[0][1], 46), (64, a[1][1], 66),
                (84, b[0][0], 87), (106, b[1][0], 109),
            ]
            tile = _roll(parts[0][1], parts[0][2] + base)
            for start, piece, shift in parts[1:]:
                tile = jnp.where(lane >= start, _roll(piece, shift + base), tile)
            out_ref[d, 2 * t] = trimmed(tile, d, low)
            parts = [
                (0, b[0][1], 2), (20, b[1][1], 22), (40, c[0][0], 43), (62, c[1][0], 65),
                (84, c[0][1], 86), (104, c[1][1], 106),
            ]
            tile = _roll(parts[0][1], parts[0][2] + base)
            for start, piece, shift in parts[1:]:
                tile = jnp.where(lane >= start, _roll(piece, shift + base), tile)
            out_ref[d, 2 * t + 1] = trimmed(tile, d, high)
        return 0

    lax.fori_loop(0, TRI, triple, 0)
    which = which_ref[0]
    other = jnp.maximum(which - 1, 0)
    coef = [jnp.where(which == 0, mean_ref[p], fluct_ref[other, p]) for p in range(2)]
    offset = lane % GW - 3
    for d in range(PARTS):
        tile = jnp.where(lane >= GW, _roll(coef[1], 25 - ZW * d), _roll(coef[0], 3 - ZW * d))
        out_ref[d, ROWS - 1] = trimmed(tile, d, offset)


def _far_kernel(block_ref, right_ref, left_ref):
    lane = _lane()

    def per_block(s, _):
        for plane, out_ref in ((1, right_ref), (0, left_ref)):
            for half in range(2):
                tile = None
                for q in range(8):
                    m = 8 * half + q
                    t, r = divmod(m, 3)
                    row = ROWS - 1 if m == 15 else 2 * t + (r == 2)
                    start = 3 + GW * plane + (0 if m == 15 else (MW * r) % 128)
                    piece = _roll(block_ref[s, row], 16 * q - start)
                    tile = piece if tile is None else jnp.where(lane >= 16 * q, piece, tile)
                out_ref[s, half] = tile
        return 0

    lax.fori_loop(0, PARTS, per_block, 0)


def _sweep_kernel(
    j1_ref, j2_ref, c1_ref, c2_ref, table_ref, own_ref, left_ref, right_ref, left2_ref, right2_ref,
    out_ref, s0_ref, s1_ref, t0_ref, ls_ref, f_ref, a0_ref, a1_ref, b_ref,
):
    lane = _lane()

    def row(at):
        return jnp.broadcast_to(table_ref[pl.ds(at, 1), :], (Y, 128))

    y = lax.broadcasted_iota(jnp.int32, (Y, 128), 0)
    inner_up = (y > 0).astype(jnp.float32)
    inner_down = (y < Y - 1).astype(jnp.float32)

    def along_y(x):
        return pltpu.roll(x, 1, 0) * inner_up + pltpu.roll(x, Y - 1, 0) * inner_down

    def near(x0, x1=None):
        total = along_y(x0)
        for n in range(4):
            piece = _take(x0, row(AT["near0"][n]))
            if x1 is not None:
                piece = jnp.where(row(AT["which"][n]) != 0, _take(x1, row(AT["near1"][n])), piece)
            total = total + piece
        return total

    def gathered(s, rows, index, code):
        tile = _take(own_ref[s, rows], index)
        tile = jnp.where(code == 1, _take(left_ref[s, rows], index), tile)
        return jnp.where(code == 2, _take(right_ref[s, rows], index), tile)

    def pair(s, rows, r, half, q):
        code0, code1 = row(AT["code0"]), row(AT["code1"])
        first = gathered(s, rows, row(AT["v0"][r]), code0)
        second = gathered(s, rows, row(AT["v1"][r]), code1)
        second = jnp.where(code1 == 3, _roll(left2_ref[s, half], 12 - 16 * q), second)
        second = jnp.where(code1 == 4, _roll(right2_ref[s, half], 28 - 16 * q), second)
        return first, jnp.where(lane < 44, second, 0.0)

    def unpack(s, _):
        for m in range(BLOCK):
            t, r = divmod(m, 3)
            first, second = pair(s, 2 * t + (r == 2), r, m // 8, m % 8)
            s0_ref[s * BLOCK + m] = first
            s1_ref[s * BLOCK + m] = second
            f_ref[s * BLOCK + m] = 2.0 * gathered(s, 2 * t + (r > 0), row(AT["f"][r]), row(AT["code0"]))
        first, second = pair(s, ROWS - 1, 0, 1, 7)
        a0_ref[s] = first
        a1_ref[s] = second
        b_ref[s] = 6.0 * first + near(first, second)
        return 0

    lax.fori_loop(0, PARTS, unpack, 0)
    mean = a0_ref[0]
    inside = mean > 0.0
    b_ref[TERMS] = jnp.where(inside, 1.0 / jnp.where(inside, b_ref[0], 1.0), 0.0)

    def neighbours_of(src_ref, wide):
        def body(j, _):
            ls_ref[j] = near(src_ref[j], s1_ref[j] if wide else None)
            return 0

        lax.fori_loop(0, MODES, body, 0, unroll=4)

    def sweep(src_ref, dst_ref, wide, last):
        neighbours_of(src_ref, wide)

        def body(i, _):
            mine = src_ref[i]
            u0 = a0_ref[0] * mine
            u1 = a1_ref[0] * s1_ref[i] if wide else None
            v = b_ref[0] * mine - a0_ref[0] * ls_ref[i]
            for k in range(1, TERMS):
                at = i * (TERMS - 1) + (k - 1)
                j1, j2, c1, c2 = j1_ref[at], j2_ref[at], c1_ref[at], c2_ref[at]
                m0 = c1 * src_ref[j1] + c2 * src_ref[j2]
                lm = c1 * ls_ref[j1] + c2 * ls_ref[j2]
                a0 = a0_ref[k]
                u0 = u0 + a0 * m0
                v = v + (b_ref[k] * m0 - a0 * lm)
                if wide:
                    u1 = u1 + a1_ref[k] * (c1 * s1_ref[j1] + c2 * s1_ref[j2])
            update = (f_ref[i] - v + near(u0, u1)) * b_ref[TERMS]
            dst_ref[i] = mine + 0.5 * update
            if last:
                f_ref[i] = update
            return 0

        lax.fori_loop(0, MODES, body, 0, unroll=2)

    sweep(s0_ref, t0_ref, True, False)
    sweep(t0_ref, s0_ref, False, False)
    sweep(s0_ref, t0_ref, False, True)

    def pack(d, _):
        index = row(AT["own"])
        for q in range(8):
            m = d * BLOCK + 2 * q
            tile = jnp.where(lane < 32, _take(t0_ref[m], index), _take(f_ref[m], index))
            if q < 7:
                tile = jnp.where(lane >= 64, _take(t0_ref[m + 1], index), tile)
                tile = jnp.where(lane >= 96, _take(f_ref[m + 1], index), tile)
            out_ref[d, q] = tile
        return 0

    lax.fori_loop(0, PARTS, pack, 0)


def _receive_kernel(piece_ref, solution_ref, update_ref):
    lane = _lane()

    def per_pair(q, _):
        tiles = [piece_ref[d, q] for d in range(PARTS)]
        for r in range(2):
            for n in range(4):
                tile = _roll(tiles[0], -64 * r - 16 * n)
                for d in range(1, PARTS):
                    tile = jnp.where(lane >= 16 * d, _roll(tiles[d], 16 * d - 64 * r - 16 * n), tile)
                out_ref = (solution_ref, update_ref)[n // 2]

                @pl.when(2 * q + r < BLOCK)
                def _():
                    out_ref[jnp.minimum(2 * q + r, BLOCK - 1), n % 2] = tile

        return 0

    lax.fori_loop(0, 8, per_pair, 0)


def _vmem(count):
    return [pl.BlockSpec(memory_space=pltpu.VMEM)] * count


def _smem(count):
    return [pl.BlockSpec(memory_space=pltpu.SMEM)] * count


def pattern_tables(triples, coupling):
    entries = coupling.shape[0]
    key = triples[0] * (TERMS - 1) + triples[2] - 1
    slots = lax.iota(jnp.int32, MODES * (TERMS - 1))
    code = lax.iota(jnp.int32, entries) * 128 + triples[1]
    match = key[:, None] == slots[None, :]
    low = jnp.min(jnp.where(match, code[:, None], entries * 128), axis=0)
    high = jnp.max(jnp.where(match, code[:, None], -1), axis=0)
    c1 = jnp.sum(jnp.where(code[:, None] == low[None, :], coupling[:, None], 0.0), axis=0)
    c2 = jnp.sum(jnp.where(code[:, None] == high[None, :], coupling[:, None], 0.0), axis=0)
    return low % 128, high % 128, c1, c2


def per_device(guess, source, mean_coef, fluct_coef, triples, coupling):
    f32 = jnp.float32
    which = lax.axis_index("mode").astype(jnp.int32).reshape(1)
    message = pl.pallas_call(
        _send_kernel,
        out_shape=jax.ShapeDtypeStruct((PARTS, ROWS, Y, 128), f32),
        in_specs=_smem(1) + _vmem(4),
        out_specs=_vmem(1)[0],
        name="send",
    )(which, guess, source, mean_coef, fluct_coef)
    block = lax.all_to_all(message, "mode", 0, 0, tiled=True)
    far_right, far_left = pl.pallas_call(
        _far_kernel,
        out_shape=[jax.ShapeDtypeStruct((PARTS, 2, Y, 128), f32)] * 2,
        in_specs=_vmem(1),
        out_specs=_vmem(2),
        name="far",
    )(block)
    count = lax.axis_size("space")

    def up(x, by):
        return lax.ppermute(x, "space", [(n, n + by) for n in range(count - by)])

    def down(x, by):
        return lax.ppermute(x, "space", [(n + by, n) for n in range(count - by)])

    from_left, from_right = up(block, 1), down(block, 1)
    from_left2, from_right2 = up(far_right, 2), down(far_left, 2)
    j1, j2, c1, c2 = pattern_tables(triples, coupling)
    tile = (Y, 128)
    result = pl.pallas_call(
        _sweep_kernel,
        out_shape=jax.ShapeDtypeStruct((PARTS, 8, Y, 128), f32),
        in_specs=_smem(4) + _vmem(6),
        out_specs=_vmem(1)[0],
        scratch_shapes=[pltpu.VMEM((MODES,) + tile, f32)] * 5
        + [pltpu.VMEM((TERMS,) + tile, f32)] * 2
        + [pltpu.VMEM((TERMS + 1,) + tile, f32)],
        name="sweeps",
    )(j1, j2, c1, c2, jnp.asarray(TABLE), block, from_left, from_right, from_left2, from_right2)
    pieces = lax.all_to_all(result, "mode", 0, 0, tiled=True)
    return tuple(
        pl.pallas_call(
            _receive_kernel,
            out_shape=[jax.ShapeDtypeStruct(guess.shape, f32)] * 2,
            in_specs=_vmem(1),
            out_specs=_vmem(2),
            name="receive",
        )(pieces)
    )


def solution(mesh):
    in_specs = (
        P("mode", "space", None, None),
        P("mode", "space", None, None),
        P("space", None, None),
        P(None, "space", None, None),
        P(),
        P(),
    )
    out_specs = (P("mode", "space", None, None), P("mode", "space", None, None))
    return jax.shard_map(
        per_device, mesh=mesh, in_specs=in_specs, out_specs=out_specs, check_vma=False
    )
```

time: 139 us -> 108 us (0.78)
  Pallas kernels: 0 us -> 54.5 us
  blocking collectives: 41.3 us -> 11.5 us
  waiting for transfers between devices: 32.1 us -> 8.94 us
  starting transfers between devices: 38.5 us -> 26.8 us
  other arithmetic: 15.6 us -> 4.42 us
  matrix products: 6.64 us -> 0 us
  local copies, waits for them, and re-layouts: 3.37 us -> 0.86 us
    pallas_call x0 -> x4, Pallas kernels: none -> 54.5 us  [the longest x1 43 us: per_device(): pl.pallas_call(_sweep_kernel, out_shape=jax.ShapeDtypeStruct((PARTS, 8, Y...]
    all_gather x3 -> x0, blocking collectives: 41.3 us -> none  [per_device(): piece = lax.all_gather(solution, 'mode', axis=0, tiled=True)]
    ppermute x8 -> x4, waiting for transfers between devices: 32.1 us -> 2.21 us  [the longest x2 2.13 us: down(): return lax.ppermute(x, 'space', [(n + by, n) for n in range(count - by)])]
    ppermute x8 -> x4, starting transfers between devices: 38.5 us -> 22.3 us  [the longest x2 18.5 us: down(): return lax.ppermute(x, 'space', [(n + by, n) for n in range(count - by)])]
    all_to_all x0 -> x1, blocking collectives: none -> 11.5 us  [per_device(): pieces = lax.all_to_all(result, 'mode', 0, 0, tiled=True)]
    all_to_all x0 -> x1, waiting for transfers between devices: none -> 6.73 us  [per_device(): block = lax.all_to_all(message, 'mode', 0, 0, tiled=True)]
    dot_general x4 -> x0, matrix products: 6.64 us -> none  [the longest x3 3.65 us: per_device(): jnp.dot(mixing, piece.reshape(piece.shape[0], -1), precision=lax.Precisio...]
    reshape x3 -> x0, other arithmetic: 6.56 us -> none  [per_device(): pad_sides(mixed).reshape(blocks, terms, planes + 2, rows_y + 2, rows_z + 2)]
  transfers between devices with their start and end apart: 8 -> 5, of which waited for: 6 -> 3; matrix products, arithmetic and copies ran while one was open for 5% -> 4% of each run, Pallas kernels for 0% -> 2%
where the time goes in v1:
time: 108 us
  Pallas kernels  54.5 us (50%)
  starting transfers between devices  26.8 us (25%)
  blocking collectives  11.5 us (11%)
  waiting for transfers between devices  8.94 us (8%)
  other arithmetic  4.42 us (4%)
    pallas_call x1, Pallas kernels, per_device(): pl.pallas_call(_sweep_kernel, out_shape=jax.ShapeDtypeStruct((PARTS, 8, Y...  43 us
    ppermute x2, starting transfers between devices, down(): return lax.ppermute(x, 'space', [(n + by, n) for n in range(count - by)])  18.5 us
    all_to_all x1, blocking collectives, per_device(): pieces = lax.all_to_all(result, 'mode', 0, 0, tiled=True)  11.5 us
    all_to_all x1, waiting for transfers between devices, per_device(): block = lax.all_to_all(message, 'mode', 0, 0, tiled=True)  6.73 us
    pallas_call x1, Pallas kernels, per_device(): pl.pallas_call(_receive_kernel, out_shape=[jax.ShapeDtypeStruct(guess.sha...  6.43 us
    all_to_all x1, starting transfers between devices, per_device(): block = lax.all_to_all(message, 'mode', 0, 0, tiled=True)  4.43 us
    ppermute x2, starting transfers between devices, up(): return lax.ppermute(x, 'space', [(n, n + by) for n in range(count - by)])  3.83 us
    pallas_call x1, Pallas kernels, per_device(): pl.pallas_call(_send_kernel, out_shape=jax.ShapeDtypeStruct((PARTS, ROWS,...  2.66 us
  transfers between devices with their start and end apart: 5, of which 3 were waited for; matrix products, arithmetic and copies ran while one was open for 4% of the time, Pallas kernels for 2%

profile of v1, /device:TPU:24, one launch (start us, length us, event | category | flops | bytes accessed | tf_op | source)
XLA Modules:
  0.0 107.8 jit_solution(14297943639168007285)
XLA Ops:
  0.6 2.7 %send.1 = f32[8,11,8,128]{3,2,1,0:T(8,128)} custom-call(s32[1]{0:T(128)} %bitcast.which_ref, f32[15,2,8,128]{3,2,1,0:T(8,128)} %guess_ref.1, f32[15,2,8,128]{3,2,1,0:T(8,128)} %source_ref.1, f32[2,8,128]{2,1,0:T(8,128)} %mean_ref.1, f32[7,2,8,128]{3,2,1,0:T(8,128)} %fluct_ref.1), custom_call_target="tpu_custom_call" | custom-call | tf_op jit(solution)/shard_map/send/pallas_call | solution.py:329
  3.3 0.0 copy-start.5
  3.3 0.0 copy-start.6
  3.3 4.4 %all-to-all-start = ((f32[8,11,8,128]{3,2,1,0:T(8,128)}), f32[8,11,8,128]{3,2,1,0:T(8,128)S(1)}, u32[]{:S(2)}, u32[]{:S(2)}) async-start(f32[8,11,8,128]{3,2,1,0:T(8,128)} %send.1), calls=%async_computation | async-start | bytes 720896 | tf_op jit(solution)/shard_map/all_to_all | solution.py:336
  7.7 0.0 copy-done.5
  7.7 0.1 slice_reduce_fusion
  7.8 1.7 %select_reduce_fusion.2 = (s32[840]{0:T(1024)S(1)}, s32[840]{0:T(1024)S(1)}) fusion(s32[1680]{0:T(1024)S(1)} %get-tuple-element.7, s32[1680]{0:T(1024)S(1)} %multiply_add_fusion), kind=kLoop, calls=%fused_computation.2 | loop fusion | flops 7054320 | bytes 20160 | tf_op jit(solution)/shard_map/reduce_max | solution.py:320
  9.6 6.7 %all-to-all-done.block_ref.own_ref = f32[8,11,8,128]{3,2,1,0:T(8,128)S(1)} async-done(((f32[8,11,8,128]{3,2,1,0:T(8,128)}), f32[8,11,8,128]{3,2,1,0:T(8,128)S(1)}, u32[]{:S(2)}, u32[]{:S(2)}) %all-to-all-start) | async-done | bytes 360480 | tf_op jit(solution)/shard_map/all_to_all | solution.py:336
  16.3 0.0 copy-start
  16.3 11.6 %collective-permute-start.1 = (f32[8,11,8,128]{3,2,1,0:T(8,128)S(1)}, f32[8,11,8,128]{3,2,1,0:T(8,128)S(1)}, u32[]{:S(2)}, u32[]{:S(2)}) collective-permute-start(f32[8,11,8,128]{3,2,1,0:T(8,128)S(1)} %all-to-all-done.block_ref.own_ref), channel_id=1, source_target_pairs={{8,0},{16,8},{24,16},{32,24},{40,32},{48,40},{56,48},{64,56},{72,6... | collective-permute-start | bytes 1081352 | tf_op jit(solution)/shard_map/ppermute | solution.py:350
  27.9 1.9 %collective-permute-start = (f32[8,11,8,128]{3,2,1,0:T(8,128)S(1)}, f32[8,11,8,128]{3,2,1,0:T(8,128)S(1)}, u32[]{:S(2)}, u32[]{:S(2)}) collective-permute-start(f32[8,11,8,128]{3,2,1,0:T(8,128)S(1)} %all-to-all-done.block_ref.own_ref), channel_id=1, source_target_pairs={{0,8},{8,16},{16,24},{24,32},{32,40},{40,48},{48,56},{56,64},{64,7... | collective-permute-start | bytes 1081352 | tf_op jit(solution)/shard_map/ppermute | solution.py:347
  29.8 0.0 copy-done.6
  29.8 2.0 %select_reduce_fusion = (f32[840]{0:T(1024)}, f32[840]{0:T(1024)}) fusion(s32[840]{0:T(1024)S(1)} %get-tuple-element.10, f32[1680]{0:T(1024)S(1)} %copy-done.6, s32[1680]{0:T(1024)S(1)} %multiply_add_fusion, s32[840]{0:T(1024)S(1)} %get-tuple-element.11), kind=kLoop, calls=%fused_computation | loop fusion | flops 8465520 | bytes 26880 | tf_op jit(solution)/shard_map/reduce_sum | solution.py:322
  31.8 0.0 copy-done
  31.8 2.4 %far.1 = (f32[8,2,8,128]{3,2,1,0:T(8,128)}, f32[8,2,8,128]{3,2,1,0:T(8,128)}) custom-call(f32[8,11,8,128]{3,2,1,0:T(8,128)} %copy-done), custom_call_target="tpu_custom_call" | custom-call | tf_op jit(solution)/shard_map/far/pallas_call | solution.py:337
  34.3 1.9 %collective-permute-start.2 = (f32[8,2,8,128]{3,2,1,0:T(8,128)}, f32[8,2,8,128]{3,2,1,0:T(8,128)S(1)}, u32[]{:S(2)}, u32[]{:S(2)}) collective-permute-start(f32[8,2,8,128]{3,2,1,0:T(8,128)} %get-tuple-element.4), channel_id=1, source_target_pairs={{0,16},{8,24},{16,32},{24,40},{32,48},{40,56},{48,64},{56,72},{64,... | collective-permute-start | bytes 196616 | tf_op jit(solution)/shard_map/ppermute | solution.py:347
  36.2 6.9 %collective-permute-start.3 = (f32[8,2,8,128]{3,2,1,0:T(8,128)}, f32[8,2,8,128]{3,2,1,0:T(8,128)S(1)}, u32[]{:S(2)}, u32[]{:S(2)}) collective-permute-start(f32[8,2,8,128]{3,2,1,0:T(8,128)} %get-tuple-element.5), channel_id=1, source_target_pairs={{16,0},{24,8},{32,16},{40,24},{48,32},{56,40},{64,48},{72,56},{80,... | collective-permute-start | bytes 196616 | tf_op jit(solution)/shard_map/ppermute | solution.py:350
  43.1 0.6 add_select_fusion
  43.7 0.1 collective-permute-done.2.left2_ref
  43.8 0.0 copy-start.3
  43.8 2.1 %collective-permute-done.3.right2_ref = f32[8,2,8,128]{3,2,1,0:T(8,128)S(1)} collective-permute-done((f32[8,2,8,128]{3,2,1,0:T(8,128)}, f32[8,2,8,128]{3,2,1,0:T(8,128)S(1)}, u32[]{:S(2)}, u32[]{:S(2)}) %collective-permute-start.3) | collective-permute-done | bytes 65568 | tf_op jit(solution)/shard_map/ppermute | solution.py:350
  45.9 0.0 copy-start.4
  45.9 0.0 collective-permute-done.1.right_ref
  46.0 0.0 collective-permute-done.left_ref
  46.0 0.0 copy-start.2
  46.0 0.0 copy-done.3
  46.0 0.6 copy-done.4
  46.6 0.1 copy-done.1
  46.7 0.1 copy-done.2
  46.8 43.0 %sweeps.1 = f32[8,8,8,128]{3,2,1,0:T(8,128)} custom-call(s32[840]{0:T(1024)} %get-tuple-element.13.j1_ref, s32[840]{0:T(1024)} %get-tuple-element.12.j2_ref, f32[840]{0:T(1024)} %get-tuple-element.9.c1_ref, f32[840]{0:T(1024)} %get-tuple-element.8.c2_ref, s32[24,128]{1,0:T(8,128)} %constant.41.clone.table_ref, f32[8,11,8,128]{3,2,1,0:T(8,128)} %copy-done, ...), custom_call_target="tpu_custom_call" | custom-call | tf_op jit(solution)/shard_map/sweeps/pallas_call | solution.py:356
  89.8 11.5 %all_to_all.10.piece_ref = f32[8,8,8,128]{3,2,1,0:T(8,128)} all-to-all(f32[8,8,8,128]{3,2,1,0:T(8,128)} %sweeps.1), channel_id=1, replica_groups=mesh['space'=64,'mode'=8] {'mode'}, dimensions={0} | all-to-all | bytes 524288 | tf_op jit(solution)/shard_map/all_to_all | solution.py:366
  101.3 6.4 %receive.1 = (f32[15,2,8,128]{3,2,1,0:T(8,128)}, f32[15,2,8,128]{3,2,1,0:T(8,128)}) custom-call(f32[8,8,8,128]{3,2,1,0:T(8,128)} %all_to_all.10.piece_ref), custom_call_target="tpu_custom_call" | custom-call | tf_op jit(solution)/shard_map/receive/pallas_call | solution.py:368
  (2 shorter events, 0.0 us)
Async XLA Ops:
  3.3 4.4 %copy-start.5 = (s32[3,1680]{1,0:T(4,128)S(1)}, s32[3,1680]{1,0:T(4,128)}, u32[]{:S(2)}) copy-start(s32[3,1680]{1,0:T(4,128)} %param.11) | copy-start | bytes 60484
  3.3 26.5 %copy-start.6 = (f32[1680]{0:T(1024)S(1)}, f32[1680]{0:T(1024)}, u32[]{:S(2)}) copy-start(f32[1680]{0:T(1024)} %param.12) | copy-start | bytes 20164
  3.3 13.0 %all-to-all-start = ((f32[8,11,8,128]{3,2,1,0:T(8,128)}), f32[8,11,8,128]{3,2,1,0:T(8,128)S(1)}, u32[]{:S(2)}, u32[]{:S(2)}) async-start(f32[8,11,8,128]{3,2,1,0:T(8,128)} %send.1), calls=%async_computation | async-start | bytes 720896 | tf_op jit(solution)/shard_map/all_to_all | solution.py:336
  16.3 15.5 %copy-start = (f32[8,11,8,128]{3,2,1,0:T(8,128)}, f32[8,11,8,128]{3,2,1,0:T(8,128)S(1)}, u32[]{:S(2)}) copy-start(f32[8,11,8,128]{3,2,1,0:T(8,128)S(1)} %all-to-all-done.block_ref.own_ref) | copy-start | bytes 1081348
  16.3 29.7 %collective-permute-start.1 = (f32[8,11,8,128]{3,2,1,0:T(8,128)S(1)}, f32[8,11,8,128]{3,2,1,0:T(8,128)S(1)}, u32[]{:S(2)}, u32[]{:S(2)}) collective-permute-start(f32[8,11,8,128]{3,2,1,0:T(8,128)S(1)} %all-to-all-done.block_ref.own_ref), channel_id=1, source_target_pairs={{8,0},{16,8},{24,16},{32,24},{40,32},{48,40},{56,48},{64,56},{72,6... | collective-permute-start | bytes 1081352 | tf_op jit(solution)/shard_map/ppermute | solution.py:350
  27.9 18.1 %collective-permute-start = (f32[8,11,8,128]{3,2,1,0:T(8,128)S(1)}, f32[8,11,8,128]{3,2,1,0:T(8,128)S(1)}, u32[]{:S(2)}, u32[]{:S(2)}) collective-permute-start(f32[8,11,8,128]{3,2,1,0:T(8,128)S(1)} %all-to-all-done.block_ref.own_ref), channel_id=1, source_target_pairs={{0,8},{8,16},{16,24},{24,32},{32,40},{40,48},{48,56},{56,64},{64,7... | collective-permute-start | bytes 1081352 | tf_op jit(solution)/shard_map/ppermute | solution.py:347
  34.3 9.5 %collective-permute-start.2 = (f32[8,2,8,128]{3,2,1,0:T(8,128)}, f32[8,2,8,128]{3,2,1,0:T(8,128)S(1)}, u32[]{:S(2)}, u32[]{:S(2)}) collective-permute-start(f32[8,2,8,128]{3,2,1,0:T(8,128)} %get-tuple-element.4), channel_id=1, source_target_pairs={{0,16},{8,24},{16,32},{24,40},{32,48},{40,56},{48,64},{56,72},{64,... | collective-permute-start | bytes 196616 | tf_op jit(solution)/shard_map/ppermute | solution.py:347
  36.2 9.8 %collective-permute-start.3 = (f32[8,2,8,128]{3,2,1,0:T(8,128)}, f32[8,2,8,128]{3,2,1,0:T(8,128)S(1)}, u32[]{:S(2)}, u32[]{:S(2)}) collective-permute-start(f32[8,2,8,128]{3,2,1,0:T(8,128)} %get-tuple-element.5), channel_id=1, source_target_pairs={{16,0},{24,8},{32,16},{40,24},{48,32},{56,40},{64,48},{72,56},{80,... | collective-permute-start | bytes 196616 | tf_op jit(solution)/shard_map/ppermute | solution.py:350
  43.8 2.2 %copy-start.3 = (f32[8,2,8,128]{3,2,1,0:T(8,128)}, f32[8,2,8,128]{3,2,1,0:T(8,128)S(1)}, u32[]{:S(2)}) copy-start(f32[8,2,8,128]{3,2,1,0:T(8,128)S(1)} %collective-permute-done.2.left2_ref) | copy-start | bytes 196612
  45.9 0.6 copy-start.4
  46.0 0.7 copy-start.1
  46.0 0.9 copy-start.2

commit v2 on v0

v2 whole, which is shorter than its diff:
```python
import jax
import jax.numpy as jnp
import numpy as np
from jax import lax
from jax.experimental import pallas as pl
from jax.experimental.pallas import tpu as pltpu
from jax.sharding import Mesh
from jax.sharding import PartitionSpec as P

ITERS = 3
SLABS = 2
PARTS = 8
GROUP = SLABS * PARTS
BLOCK = 15
MODES = 120
TERMS = 8
Y, Z = 8, 128
ZW = 8
PW = 14
SLOT = 64
F32 = jnp.float32


def _lane_of(plane, z):
    if plane == -3:
        return 112 + z
    if plane == 6:
        return 120 + z
    return PW * (plane + 2) + z + 3


def _near_matrix():
    cells = {}
    for plane in range(-2, 6):
        for z in range(-3, 11):
            cells[plane, z] = _lane_of(plane, z)
    for plane in (-3, 6):
        for z in range(ZW):
            cells[plane, z] = _lane_of(plane, z)
    near = np.zeros((128, 128), np.float32)
    for (plane, z), lane in cells.items():
        for cell in ((plane + 1, z), (plane - 1, z), (plane, z + 1), (plane, z - 1)):
            if cell in cells:
                near[cells[cell], lane] = 1.0
    return np.concatenate([near] * 3, axis=0)


G_PARTS = ((-2, 12), (-1, 10), (0, 8))
F_PARTS = ((-1, 10), (0, 8))
G_FROM = {"right": (PW + 1, 2, 56), "left": (1, PW + 2, 56)}
F_FROM = {"right": (3 * PW + 2, 2 * PW + 3), "left": (2 * PW + 2, 3 * PW + 3)}


def _tables():
    rows, at = [], {}

    def add(name, fill):
        row = np.zeros(128, np.int32)
        for lane, value in fill:
            row[lane] = value
        at[name] = len(rows)
        rows.append(row)

    def f_place(j):
        if j < 6:
            return (2, 18 * j), (2, 18 * j + 10)
        return (2, 108 + 10 * (j - 6)), (j - 6, 120)

    for way in ("right", "left"):
        index = [[], [], []]
        source = [[], [], []]
        for j in range(8):
            base, row = SLOT * (j % 2), j // 2
            lane = 30 * (j % 4)
            for start, (_, width) in zip(G_FROM[way], G_PARTS):
                for t in range(width):
                    index[j // 4].append((lane, base + start + t))
                    source[j // 4].append((lane, row))
                    lane += 1
            for start, (_, width), (tile, lane) in zip(F_FROM[way], F_PARTS, f_place(j)):
                for t in range(width):
                    index[tile].append((lane + t, base + start + t))
                    source[tile].append((lane + t, row))
        for w in range(3):
            add(("pack", way, w), index[w])
            add(("from", w), source[w])
    sides = ((-1, -2, -3), (4, 5, 6))
    for pos in range(4):
        fill = []
        for planes in sides:
            lane = 30 * pos
            for plane, (low, width) in zip(planes, G_PARTS):
                for t in range(width):
                    fill.append((_lane_of(plane, low + t), lane))
                    lane += 1
        add(("g", pos), fill)
    for j in range(8):
        fill = []
        for planes in sides:
            for plane, (low, width), (_, lane) in zip(planes, F_PARTS, f_place(j)):
                fill += [(_lane_of(plane, low + t), lane + t) for t in range(width)]
        add(("f", j), fill)
    for slab in range(SLABS):
        fill = []
        for lane in range(128):
            part, z = lane % 32 // ZW, lane % ZW
            home = _lane_of(SLABS * slab + part % 2, z)
            fill.append((lane, (home + SLOT * (part // 2)) % 128))
        add(("own", slab), fill)
    while len(rows) % 8:
        rows.append(np.zeros(128, np.int32))
    return np.stack(rows), at


TABLE, AT = _tables()
NEAR = _near_matrix()


def _take(tile, index):
    return jnp.take_along_axis(tile, index, axis=1, mode="promise_in_bounds")


def _lane():
    return lax.broadcasted_iota(jnp.int32, (Y, 128), 1)


def _roll(tile, amount):
    amount %= 128
    return pltpu.roll(tile, amount, 1) if amount else tile


def _send_kernel(which_ref, guess_ref, source_ref, mean_ref, fluct_ref, out_ref):
    lane = _lane()
    off = lane % SLOT % PW - 3
    which = which_ref[0]
    other = jnp.maximum(which - 1, 0)
    for t in range(PARTS):
        pieces = []
        for r in range(2):
            m = 2 * t + r
            if m < BLOCK:
                four = (guess_ref[m, 0], guess_ref[m, 1], source_ref[m, 0], source_ref[m, 1])
            else:
                four = tuple(jnp.where(which == 0, mean_ref[p], fluct_ref[other, p]) for p in range(2))
            for n, piece in enumerate(four):
                start = SLOT * r + PW * n
                pieces.append((start, _roll(piece, start + 3)))
        for q in range(GROUP):
            shifted = (lane - ZW * q) & 127
            tile = pieces[0][1]
            for start, piece in pieces[1:]:
                tile = jnp.where(shifted >= start, piece, tile)
            tile = _roll(tile, -ZW * q)
            if q == 0:
                tile = jnp.where(off < 0, 0.0, tile)
            if q == GROUP - 1:
                tile = jnp.where(off >= ZW, 0.0, tile)
            out_ref[q, t] = tile


def _halo_kernel(table_ref, block_ref, right_ref, left_ref):
    spare = _lane() % SLOT >= 4 * PW

    def row(name):
        return jnp.broadcast_to(table_ref[pl.ds(AT[name], 1), :], (Y, 128))

    for way, out_ref in (("right", right_ref), ("left", left_ref)):
        home, away, shift = (PARTS, 0, 56 - 17) if way == "right" else (0, PARTS, 56 - 3)
        for half in range(2 * PARTS):
            md, h = divmod(half, 2)
            merged = []
            for t in range(4 * h, 4 * h + 4):
                merged.append(jnp.where(spare, _roll(block_ref[away + md, t], shift), block_ref[home + md, t]))
            for w, sources in ((0, (0, 1, 3)), (1, (2, 3)), (2, (0, 1, 2, 3))):
                index, code = row(("pack", way, w)), row(("from", w))
                tile = _take(merged[sources[0]], index)
                for t in sources[1:]:
                    tile = jnp.where(code == t, _take(merged[t], index), tile)
                out_ref[md, h, w] = tile


def _sweep_kernel(
    jj_ref, c1_ref, c2_ref, table_ref, near_ref, own_ref, left_ref, right_ref,
    out_ref, sl_ref, u_ref, w_ref, f_ref, up_ref, a_ref, b_ref,
):
    lane = _lane()
    y = lax.broadcasted_iota(jnp.int32, (1, Y, 128), 1)
    inner_up = (y > 0).astype(F32)
    inner_down = (y < Y - 1).astype(F32)

    def row(name):
        return jnp.broadcast_to(table_ref[pl.ds(AT[name], 1), :], (Y, 128))

    def near(x):
        high = x.astype(jnp.bfloat16)
        rest = x - high.astype(F32)
        middle = rest.astype(jnp.bfloat16)
        low = (rest - middle.astype(F32)).astype(jnp.bfloat16)
        total = jnp.dot(
            jnp.concatenate([high, middle, low], axis=1), near_ref[...], preferred_element_type=F32
        )
        tiles = x.reshape(-1, Y, 128)
        along = pltpu.roll(tiles, 1, 1) * inner_up + pltpu.roll(tiles, Y - 1, 1) * inner_down
        return total + along.reshape(x.shape)

    from_left = (lane < 28) | ((lane >= 112) & (lane < 120))
    first = lane < 56
    second = (lane >= 56) & (lane < 84)

    def joined(left, right, a, b):
        tile = jnp.where(from_left, left, right)
        tile = jnp.where((lane >= 28) & first, a, tile)
        return jnp.where(second, b, tile)

    def f_parts(ref, md, h, j, index):
        tile = _take(ref[md, h, 2], index)
        if j >= 6:
            far = (lane < 14) | (lane >= 98)
            tile = jnp.where(far, _take(ref[md, h, j - 6], index), tile)
        return tile

    def unpack(md, _):
        for s in range(BLOCK + 1):
            t, r = divmod(s, 2)
            h, j = divmod(s, 8)
            a, b = own_ref[md, t], own_ref[PARTS + md, t]
            index = row(("g", j % 4))
            tile = joined(
                _take(left_ref[md, h, j // 4], index),
                _take(right_ref[md, h, j // 4], index),
                _roll(a, 28 - SLOT * r),
                _roll(b, 56 - SLOT * r),
            )
            if s == BLOCK:
                a_ref[pl.ds(md * Y, Y), :] = tile
                continue
            sl_ref[pl.ds((md * BLOCK + s) * 16, Y), :] = tile
            index = row(("f", j))
            f_ref[pl.ds((md * BLOCK + s) * Y, Y), :] = 2.0 * joined(
                f_parts(left_ref, md, h, j, index),
                f_parts(right_ref, md, h, j, index),
                _roll(a, -SLOT * r),
                _roll(b, 28 - SLOT * r),
            )
        return 0

    lax.fori_loop(0, PARTS, unpack, 0)
    b_ref[pl.ds(0, TERMS * Y), :] = 6.0 * a_ref[...] + near(a_ref[...])
    inside = a_ref[pl.ds(0, Y), :] > 0.0
    scale = jnp.where(inside, 1.0 / jnp.where(inside, b_ref[pl.ds(0, Y), :], 1.0), 0.0)

    chunk = 24

    def sweep(_, carry):
        for first_mode in range(0, MODES, chunk):
            x = jnp.concatenate([sl_ref[16 * j : 16 * j + Y] for j in range(first_mode, first_mode + chunk)])
            x = near(x)
            for n in range(chunk):
                sl_ref[16 * (first_mode + n) + Y : 16 * (first_mode + n) + 16] = x[Y * n : Y * n + Y]

        def mix(i, _):
            mine = sl_ref[pl.ds(i * 16, Y), :]
            a, b = a_ref[0:Y], b_ref[0:Y]
            u = a * mine
            v = b * mine - a * sl_ref[pl.ds(i * 16 + Y, Y), :]
            for k in range(1, TERMS):
                at = i * (TERMS - 1) + (k - 1)
                jj, c1, c2 = jj_ref[at], c1_ref[at], c2_ref[at]
                j1 = pl.multiple_of(jj & 0xFFFF, 16)
                j2 = pl.multiple_of(jj >> 16, 16)
                m = c1 * sl_ref[pl.ds(j1, Y), :] + c2 * sl_ref[pl.ds(j2, Y), :]
                lm = c1 * sl_ref[pl.ds(j1 + Y, Y), :] + c2 * sl_ref[pl.ds(j2 + Y, Y), :]
                a, b = a_ref[Y * k : Y * k + Y], b_ref[Y * k : Y * k + Y]
                u = u + a * m
                v = v + (b * m - a * lm)
            u_ref[pl.ds(i * Y, Y), :] = u
            w_ref[pl.ds(i * Y, Y), :] = f_ref[pl.ds(i * Y, Y), :] - v
            return 0

        lax.fori_loop(0, MODES, mix, 0, unroll=4)
        for first_mode in range(0, MODES, chunk):
            rows = pl.ds(first_mode * Y, chunk * Y)
            x = (w_ref[rows, :] + near(u_ref[rows, :])).reshape(chunk, Y, 128) * scale[None]
            for n in range(chunk):
                j = first_mode + n
                up_ref[Y * j : Y * j + Y] = x[n]
                sl_ref[16 * j : 16 * j + Y] = sl_ref[16 * j : 16 * j + Y] + 0.5 * x[n]
        return carry

    lax.fori_loop(0, ITERS, sweep, 0)
    home = (lane >= 28) & (lane < 84)

    def pack(md, _):
        both = []
        for m in range(BLOCK):
            i = md * BLOCK + m
            both.append(jnp.where(home, sl_ref[pl.ds(i * 16, Y), :], _roll(up_ref[pl.ds(i * Y, Y), :], 64)))
        for slab in range(SLABS):
            index = row(("own", slab))
            for t in range(4):
                tile = _take(both[4 * t], index)
                for r in range(1, 4):
                    if 4 * t + r < BLOCK:
                        tile = jnp.where(lane >= 32 * r, _take(both[4 * t + r], index), tile)
                out_ref[slab * PARTS + md, t] = tile
        return 0

    lax.fori_loop(0, PARTS, pack, 0)


def _receive_kernel(piece_ref, solution_ref, update_ref):
    lane = _lane()
    for t in range(4):
        rolled = [_roll(piece_ref[q, t], ZW * q) for q in range(GROUP)]
        for h in range(GROUP):
            m, n = 4 * t + h // 4, h % 4
            if m >= BLOCK:
                continue
            shifted = (lane - ZW * h) & 127
            tile = rolled[0]
            for q in range(1, GROUP):
                tile = jnp.where(shifted >= ZW * q, rolled[q], tile)
            (solution_ref, update_ref)[n // 2][m, n % 2] = _roll(tile, -ZW * h)


def _vmem(count):
    return [pl.BlockSpec(memory_space=pltpu.VMEM)] * count


def _smem(count):
    return [pl.BlockSpec(memory_space=pltpu.SMEM)] * count


def pattern_tables(triples, coupling):
    entries = coupling.shape[0]
    key = triples[0] * (TERMS - 1) + triples[2] - 1
    slots = lax.iota(jnp.int32, MODES * (TERMS - 1))
    code = lax.iota(jnp.int32, entries) * 128 + triples[1]
    match = key[:, None] == slots[None, :]
    low = jnp.min(jnp.where(match, code[:, None], entries * 128), axis=0)
    high = jnp.max(jnp.where(match, code[:, None], -1), axis=0)
    c1 = jnp.sum(jnp.where(code[:, None] == low[None, :], coupling[:, None], 0.0), axis=0)
    c2 = jnp.sum(jnp.where(code[:, None] == high[None, :], coupling[:, None], 0.0), axis=0)
    return (low & 127) * 16 + (high & 127) * (16 << 16), c1, c2


def per_device(guess, source, mean_coef, fluct_coef, triples, coupling):
    tile = (Y, 128)
    table = jnp.asarray(TABLE)
    which = lax.axis_index("mode").astype(jnp.int32).reshape(1)
    message = pl.pallas_call(
        _send_kernel,
        out_shape=jax.ShapeDtypeStruct((GROUP, PARTS) + tile, F32),
        in_specs=_smem(1) + _vmem(4),
        out_specs=_vmem(1)[0],
        name="send",
    )(which, guess, source, mean_coef, fluct_coef)
    block = lax.all_to_all(message, ("slab", "mode"), 0, 0, tiled=True)
    to_right, to_left = pl.pallas_call(
        _halo_kernel,
        out_shape=[jax.ShapeDtypeStruct((PARTS, 2, 3) + tile, F32)] * 2,
        in_specs=_vmem(2),
        out_specs=_vmem(2),
        name="halo",
    )(table, block)
    count = lax.axis_size("pair")
    from_left = lax.ppermute(to_right, "pair", [(n, n + 1) for n in range(count - 1)])
    from_right = lax.ppermute(to_left, "pair", [(n + 1, n) for n in range(count - 1)])
    jj, c1, c2 = pattern_tables(triples, coupling)
    result = pl.pallas_call(
        _sweep_kernel,
        out_shape=jax.ShapeDtypeStruct((GROUP, 4) + tile, F32),
        in_specs=_smem(3) + _vmem(5),
        out_specs=_vmem(1)[0],
        scratch_shapes=[pltpu.VMEM((MODES * 16, 128), F32)]
        + [pltpu.VMEM((MODES * Y, 128), F32)] * 4
        + [pltpu.VMEM((TERMS * Y, 128), F32)] * 2,
        name="sweeps",
    )(jj, c1, c2, table, jnp.asarray(NEAR, jnp.bfloat16), block, from_left, from_right)
    pieces = lax.all_to_all(result, ("slab", "mode"), 0, 0, tiled=True)
    return tuple(
        pl.pallas_call(
            _receive_kernel,
            out_shape=[jax.ShapeDtypeStruct(guess.shape, F32)] * 2,
            in_specs=_vmem(1),
            out_specs=_vmem(2),
            name="receive",
        )(pieces)
    )


def solution(mesh):
    slabs, parts = mesh.devices.shape
    grouped = Mesh(mesh.devices.reshape(slabs // SLABS, SLABS, parts), ("pair", "slab", "mode"))
    x = ("pair", "slab")
    in_specs = (P("mode", x), P("mode", x), P(x), P(None, x), P(), P())
    out_specs = (P("mode", x), P("mode", x))
    return jax.shard_map(
        per_device, mesh=grouped, in_specs=in_specs, out_specs=out_specs, check_vma=False
    )
```

time: 139 us -> 75.7 us (0.54)
  blocking collectives: 41.3 us -> 12.6 us
  Pallas kernels: 0 us -> 23.6 us
  starting transfers between devices: 38.5 us -> 18.9 us
  waiting for transfers between devices: 32.1 us -> 13.3 us
  other arithmetic: 15.6 us -> 4.41 us
  matrix products: 6.64 us -> 0 us
  local copies, waits for them, and re-layouts: 3.37 us -> 1.47 us
    all_gather x3 -> x0, blocking collectives: 41.3 us -> none  [per_device(): piece = lax.all_gather(solution, 'mode', axis=0, tiled=True)]
    ppermute x8 -> x2, waiting for transfers between devices: 32.1 us -> 6.36 us  [the longest x1 4.19 us: per_device(): lax.ppermute(to_left, 'pair', [(n + 1, n) for n in range(count - 1)])]
    ppermute x8 -> x2, starting transfers between devices: 38.5 us -> 13 us  [the longest x1 7.87 us: per_device(): lax.ppermute(to_left, 'pair', [(n + 1, n) for n in range(count - 1)])]
    pallas_call x0 -> x4, Pallas kernels: none -> 23.6 us  [the longest x1 15 us: per_device(): pl.pallas_call(_sweep_kernel, out_shape=jax.ShapeDtypeStruct((GROUP, 4) +...]
    all_to_all x0 -> x1, blocking collectives: none -> 12.6 us  [per_device(): pieces = lax.all_to_all(result, ('slab', 'mode'), 0, 0, tiled=True)]
    all_to_all x0 -> x1, waiting for transfers between devices: none -> 6.97 us  [per_device(): block = lax.all_to_all(message, ('slab', 'mode'), 0, 0, tiled=True)]
    dot_general x4 -> x0, matrix products: 6.64 us -> none  [the longest x3 3.65 us: per_device(): jnp.dot(mixing, piece.reshape(piece.shape[0], -1), precision=lax.Precisio...]
    reshape x3 -> x0, other arithmetic: 6.56 us -> none  [per_device(): pad_sides(mixed).reshape(blocks, terms, planes + 2, rows_y + 2, rows_z + 2)]
  transfers between devices with their start and end apart: 8 -> 3, of which waited for: 6 -> 3; matrix products, arithmetic and copies ran while one was open for 5% -> 6% of each run, Pallas kernels for 0% -> 0%
where the time goes in v2:
time: 75.7 us; the launch traced here: 75 us
  Pallas kernels  23.6 us (31%)
  starting transfers between devices  18.9 us (25%)
  waiting for transfers between devices  13.3 us (18%)
  blocking collectives  12.6 us (17%)
  other arithmetic  4.41 us (6%)
  local copies, waits for them, and re-layouts  1.47 us (2%)
    pallas_call x1, Pallas kernels, per_device(): pl.pallas_call(_sweep_kernel, out_shape=jax.ShapeDtypeStruct((GROUP, 4) +...  15 us
    all_to_all x1, blocking collectives, per_device(): pieces = lax.all_to_all(result, ('slab', 'mode'), 0, 0, tiled=True)  12.6 us
    ppermute x1, starting transfers between devices, per_device(): lax.ppermute(to_left, 'pair', [(n + 1, n) for n in range(count - 1)])  7.87 us
    all_to_all x1, waiting for transfers between devices, per_device(): block = lax.all_to_all(message, ('slab', 'mode'), 0, 0, tiled=True)  6.97 us
    all_to_all x1, starting transfers between devices, per_device(): block = lax.all_to_all(message, ('slab', 'mode'), 0, 0, tiled=True)  5.89 us
    ppermute x1, starting transfers between devices, per_device(): lax.ppermute(to_right, 'pair', [(n, n + 1) for n in range(count - 1)])  5.17 us
    pallas_call x1, Pallas kernels, per_device(): pl.pallas_call(_halo_kernel, out_shape=[jax.ShapeDtypeStruct((PARTS, 2, 3...  4.24 us
    ppermute x1, waiting for transfers between devices, per_device(): lax.ppermute(to_left, 'pair', [(n + 1, n) for n in range(count - 1)])  4.19 us
  transfers between devices with their start and end apart: 3, of which 3 were waited for; matrix products, arithmetic and copies ran while one was open for 6% of the time, Pallas kernels for 0%

profile of v2, /device:TPU:24, one launch (start us, length us, event | category | flops | bytes accessed | tf_op | source)
XLA Modules:
  0.0 75.0 jit_solution(12528939658840587502)
XLA Ops:
  0.6 2.3 %send.1 = f32[16,8,8,128]{3,2,1,0:T(8,128)} custom-call(s32[1]{0:T(128)} %bitcast.which_ref, f32[15,2,8,128]{3,2,1,0:T(8,128)} %guess_ref.1, f32[15,2,8,128]{3,2,1,0:T(8,128)} %source_ref.1, f32[2,8,128]{2,1,0:T(8,128)} %mean_ref.1, f32[7,2,8,128]{3,2,1,0:T(8,128)} %fluct_ref.1), custom_call_target="tpu_custom_call" | custom-call | tf_op jit(solution)/shard_map/send/pallas_call | solution.py:351
  3.0 0.0 copy-start.3
  3.0 0.0 copy-start.4
  3.0 5.9 %all-to-all-start = ((f32[16,8,8,128]{3,2,1,0:T(8,128)}), f32[16,8,8,128]{3,2,1,0:T(8,128)S(1)}, u32[]{:S(2)}, u32[]{:S(2)}) async-start(f32[16,8,8,128]{3,2,1,0:T(8,128)} %send.1), calls=%async_computation | async-start | bytes 1048576 | tf_op jit(solution)/shard_map/all_to_all | solution.py:358
  8.9 0.0 copy-done.3
  8.9 0.1 slice_reduce_fusion
  9.0 1.7 %select_reduce_fusion.3 = (s32[840]{0:T(1024)S(1)}, s32[840]{0:T(1024)S(1)}) fusion(s32[1680]{0:T(1024)S(1)} %get-tuple-element.7, s32[1680]{0:T(1024)S(1)} %multiply_add_fusion), kind=kLoop, calls=%fused_computation.3 | loop fusion | flops 7054320 | bytes 20160 | tf_op jit(solution)/shard_map/reduce_min | solution.py:340
  10.7 0.0 copy-done.4
  10.7 2.0 %select_reduce_fusion = (f32[840]{0:T(1024)}, f32[840]{0:T(1024)}) fusion(s32[840]{0:T(1024)S(1)} %get-tuple-element.11, f32[1680]{0:T(1024)S(1)} %copy-done.4, s32[1680]{0:T(1024)S(1)} %multiply_add_fusion, s32[840]{0:T(1024)S(1)} %get-tuple-element.10), kind=kLoop, calls=%fused_computation | loop fusion | flops 8465520 | bytes 26880 | tf_op jit(solution)/shard_map/reduce_sum | solution.py:343
  12.7 7.0 %all-to-all-done.block_ref.own_ref = f32[16,8,8,128]{3,2,1,0:T(8,128)S(1)} async-done(((f32[16,8,8,128]{3,2,1,0:T(8,128)}), f32[16,8,8,128]{3,2,1,0:T(8,128)S(1)}, u32[]{:S(2)}, u32[]{:S(2)}) %all-to-all-start) | async-done | bytes 524320 | tf_op jit(solution)/shard_map/all_to_all | solution.py:358
  19.7 0.0 copy-start
  19.7 0.8 %copy-done = f32[16,8,8,128]{3,2,1,0:T(8,128)} copy-done((f32[16,8,8,128]{3,2,1,0:T(8,128)}, f32[16,8,8,128]{3,2,1,0:T(8,128)S(1)}, u32[]{:S(2)}) %copy-start) | copy-done | bytes 524312
  20.5 4.2 %halo.1 = (f32[8,2,3,8,128]{4,3,2,1,0:T(8,128)}, f32[8,2,3,8,128]{4,3,2,1,0:T(8,128)}) custom-call(s32[32,128]{1,0:T(8,128)} %constant.30.clone.table_ref, f32[16,8,8,128]{3,2,1,0:T(8,128)} %copy-done), custom_call_target="tpu_custom_call" | custom-call | tf_op jit(solution)/shard_map/halo/pallas_call | solution.py:359
  24.7 5.2 %collective-permute-start = (f32[8,2,3,8,128]{4,3,2,1,0:T(8,128)}, f32[8,2,3,8,128]{4,3,2,1,0:T(8,128)S(1)}, u32[]{:S(2)}, u32[]{:S(2)}) collective-permute-start(f32[8,2,3,8,128]{4,3,2,1,0:T(8,128)} %get-tuple-element.4), channel_id=1, source_target_pairs={{0,16},{16,32},{32,48},{48,64},{64,80},{80,96},{96,112},{112,128},... | collective-permute-start | bytes 589832 | tf_op jit(solution)/shard_map/ppermute | solution.py:367
  29.9 7.9 %collective-permute-start.1 = (f32[8,2,3,8,128]{4,3,2,1,0:T(8,128)}, f32[8,2,3,8,128]{4,3,2,1,0:T(8,128)S(1)}, u32[]{:S(2)}, u32[]{:S(2)}) collective-permute-start(f32[8,2,3,8,128]{4,3,2,1,0:T(8,128)} %get-tuple-element.5), channel_id=1, source_target_pairs={{16,0},{32,16},{48,32},{64,48},{80,64},{96,80},{112,96},{128,112},... | collective-permute-start | bytes 589832 | tf_op jit(solution)/shard_map/ppermute | solution.py:368
  37.8 0.6 multiply_add_fusion.1.jj_ref
  38.4 2.2 %collective-permute-done.left_ref = f32[8,2,3,8,128]{4,3,2,1,0:T(8,128)S(1)} collective-permute-done((f32[8,2,3,8,128]{4,3,2,1,0:T(8,128)}, f32[8,2,3,8,128]{4,3,2,1,0:T(8,128)S(1)}, u32[]{:S(2)}, u32[]{:S(2)}) %collective-permute-start) | collective-permute-done | bytes 196640 | tf_op jit(solution)/shard_map/ppermute | solution.py:367
  40.5 0.0 copy-start.1
  40.5 4.2 %collective-permute-done.1.right_ref = f32[8,2,3,8,128]{4,3,2,1,0:T(8,128)S(1)} collective-permute-done((f32[8,2,3,8,128]{4,3,2,1,0:T(8,128)}, f32[8,2,3,8,128]{4,3,2,1,0:T(8,128)S(1)}, u32[]{:S(2)}, u32[]{:S(2)}) %collective-permute-start.1) | collective-permute-done | bytes 196640 | tf_op jit(solution)/shard_map/ppermute | solution.py:368
  44.7 0.0 copy-start.2
  44.7 0.0 copy-done.1
  44.7 0.7 copy-done.2
  45.4 15.0 %sweeps.1 = f32[16,4,8,128]{3,2,1,0:T(8,128)} custom-call(s32[840]{0:T(1024)} %multiply_add_fusion.1.jj_ref, f32[840]{0:T(1024)} %get-tuple-element.9.c1_ref, f32[840]{0:T(1024)} %get-tuple-element.8.c2_ref, s32[32,128]{1,0:T(8,128)} %constant.30.clone.table_ref, bf16[384,128]{1,0:T(8,128)(2,1)} %constant.31.clone.near_ref, f32[16,8,8,128]{3,2,1,0:T(8,128)} %copy-done, ...), custom_call_target="tpu_custom_call" | custom-call | tf_op jit(solution)/shard_map/sweeps/pallas_call | solution.py:370
  60.4 12.6 %all_to_all.10.piece_ref = f32[16,4,8,128]{3,2,1,0:T(8,128)} all-to-all(f32[16,4,8,128]{3,2,1,0:T(8,128)} %sweeps.1), channel_id=1, replica_groups=mesh['pair'=32,'slab'=2,'mode'=8] {'slab','mode'}, dimensions={0} | all-to-all | bytes 524288 | tf_op jit(solution)/shard_map/all_to_all | solution.py:380
  73.0 2.0 %receive.1 = (f32[15,2,8,128]{3,2,1,0:T(8,128)}, f32[15,2,8,128]{3,2,1,0:T(8,128)}) custom-call(f32[16,4,8,128]{3,2,1,0:T(8,128)} %all_to_all.10.piece_ref), custom_call_target="tpu_custom_call" | custom-call | tf_op jit(solution)/shard_map/receive/pallas_call | solution.py:382
  (1 shorter events, 0.0 us)
Async XLA Ops:
  3.0 5.9 %copy-start.3 = (s32[3,1680]{1,0:T(4,128)S(1)}, s32[3,1680]{1,0:T(4,128)}, u32[]{:S(2)}) copy-start(s32[3,1680]{1,0:T(4,128)} %param.12) | copy-start | bytes 60484
  3.0 7.7 %copy-start.4 = (f32[1680]{0:T(1024)S(1)}, f32[1680]{0:T(1024)}, u32[]{:S(2)}) copy-start(f32[1680]{0:T(1024)} %param.13) | copy-start | bytes 20164
  3.0 16.7 %all-to-all-start = ((f32[16,8,8,128]{3,2,1,0:T(8,128)}), f32[16,8,8,128]{3,2,1,0:T(8,128)S(1)}, u32[]{:S(2)}, u32[]{:S(2)}) async-start(f32[16,8,8,128]{3,2,1,0:T(8,128)} %send.1), calls=%async_computation | async-start | bytes 1048576 | tf_op jit(solution)/shard_map/all_to_all | solution.py:358
  19.7 0.8 %copy-start = (f32[16,8,8,128]{3,2,1,0:T(8,128)}, f32[16,8,8,128]{3,2,1,0:T(8,128)S(1)}, u32[]{:S(2)}) copy-start(f32[16,8,8,128]{3,2,1,0:T(8,128)S(1)} %all-to-all-done.block_ref.own_ref) | copy-start | bytes 1572868
  24.7 15.8 %collective-permute-start = (f32[8,2,3,8,128]{4,3,2,1,0:T(8,128)}, f32[8,2,3,8,128]{4,3,2,1,0:T(8,128)S(1)}, u32[]{:S(2)}, u32[]{:S(2)}) collective-permute-start(f32[8,2,3,8,128]{4,3,2,1,0:T(8,128)} %get-tuple-element.4), channel_id=1, source_target_pairs={{0,16},{16,32},{32,48},{48,64},{64,80},{80,96},{96,112},{112,128},... | collective-permute-start | bytes 589832 | tf_op jit(solution)/shard_map/ppermute | solution.py:367
  29.9 14.8 %collective-permute-start.1 = (f32[8,2,3,8,128]{4,3,2,1,0:T(8,128)}, f32[8,2,3,8,128]{4,3,2,1,0:T(8,128)S(1)}, u32[]{:S(2)}, u32[]{:S(2)}) collective-permute-start(f32[8,2,3,8,128]{4,3,2,1,0:T(8,128)} %get-tuple-element.5), channel_id=1, source_target_pairs={{16,0},{32,16},{48,32},{64,48},{80,64},{96,80},{112,96},{128,112},... | collective-permute-start | bytes 589832 | tf_op jit(solution)/shard_map/ppermute | solution.py:368
  40.5 4.2 %copy-start.1 = (f32[8,2,3,8,128]{4,3,2,1,0:T(8,128)}, f32[8,2,3,8,128]{4,3,2,1,0:T(8,128)S(1)}, u32[]{:S(2)}) copy-start(f32[8,2,3,8,128]{4,3,2,1,0:T(8,128)S(1)} %collective-permute-done.left_ref) | copy-start | bytes 589828
  44.7 0.7 copy-start.2

commit v3 on v2

--- a/solution.py
+++ b/solution.py
@@ -1,3 +1,5 @@
+import functools
+
 import jax
 import jax.numpy as jnp
 import numpy as np
@@ -158,29 +160,44 @@
             out_ref[q, t] = tile
 
 
-def _halo_kernel(table_ref, block_ref, right_ref, left_ref):
+def _halo_kernel(way, table_ref, block_ref, out_ref):
     spare = _lane() % SLOT >= 4 * PW
-
-    def row(name):
-        return jnp.broadcast_to(table_ref[pl.ds(AT[name], 1), :], (Y, 128))
-
-    for way, out_ref in (("right", right_ref), ("left", left_ref)):
-        home, away, shift = (PARTS, 0, 56 - 17) if way == "right" else (0, PARTS, 56 - 3)
-        for half in range(2 * PARTS):
-            md, h = divmod(half, 2)
-            merged = []
-            for t in range(4 * h, 4 * h + 4):
-                merged.append(jnp.where(spare, _roll(block_ref[away + md, t], shift), block_ref[home + md, t]))
-            for w, sources in ((0, (0, 1, 3)), (1, (2, 3)), (2, (0, 1, 2, 3))):
-                index, code = row(("pack", way, w)), row(("from", w))
-                tile = _take(merged[sources[0]], index)
+    home, away, shift = (PARTS, 0, 56 - 17) if way == "right" else (0, PARTS, 56 - 3)
+    merged = [
+        [
+            jnp.where(spare, _roll(block_ref[away + md, t], shift), block_ref[home + md, t])
+            for t in range(PARTS)
+        ]
+        for md in range(PARTS)
+    ]
+    for w, sources in ((0, (0, 1, 3)), (1, (2, 3)), (2, (0, 1, 2, 3))):
+        index = jnp.broadcast_to(table_ref[pl.ds(AT["pack", way, w], 1), :], (Y, 128))
+        code = jnp.broadcast_to(table_ref[pl.ds(AT["from", w], 1), :], (Y, 128))
+        for md in range(PARTS):
+            for h in range(2):
+                tile = _take(merged[md][4 * h + sources[0]], index)
                 for t in sources[1:]:
-                    tile = jnp.where(code == t, _take(merged[t], index), tile)
+                    tile = jnp.where(code == t, _take(merged[md][4 * h + t], index), tile)
                 out_ref[md, h, w] = tile
 
 
+def _own_kernel(block_ref, s_ref, f_ref, a_ref):
+    lane = _lane()
+    first = lane < 56
+    for md in range(PARTS):
+        for s in range(BLOCK + 1):
+            t, r = divmod(s, 2)
+            a, b = block_ref[md, t], block_ref[PARTS + md, t]
+            tile = jnp.where(first, _roll(a, 28 - SLOT * r), _roll(b, 56 - SLOT * r))
+            if s == BLOCK:
+                a_ref[md] = tile
+                continue
+            s_ref[md * BLOCK + s] = tile
+            f_ref[md * BLOCK + s] = jnp.where(first, _roll(a, -SLOT * r), _roll(b, 28 - SLOT * r))
+
+
 def _sweep_kernel(
-    jj_ref, c1_ref, c2_ref, table_ref, near_ref, own_ref, left_ref, right_ref,
+    jj_ref, c1_ref, c2_ref, table_ref, near_ref, own_s_ref, own_f_ref, own_a_ref, left_ref, right_ref,
     out_ref, sl_ref, u_ref, w_ref, f_ref, up_ref, a_ref, b_ref,
 ):
     lane = _lane()
@@ -204,47 +221,33 @@
         return total + along.reshape(x.shape)
 
     from_left = (lane < 28) | ((lane >= 112) & (lane < 120))
-    first = lane < 56
-    second = (lane >= 56) & (lane < 84)
-
-    def joined(left, right, a, b):
-        tile = jnp.where(from_left, left, right)
-        tile = jnp.where((lane >= 28) & first, a, tile)
-        return jnp.where(second, b, tile)
-
-    def f_parts(ref, md, h, j, index):
-        tile = _take(ref[md, h, 2], index)
-        if j >= 6:
-            far = (lane < 14) | (lane >= 98)
-            tile = jnp.where(far, _take(ref[md, h, j - 6], index), tile)
-        return tile
-
-    def unpack(md, _):
-        for s in range(BLOCK + 1):
-            t, r = divmod(s, 2)
-            h, j = divmod(s, 8)
-            a, b = own_ref[md, t], own_ref[PARTS + md, t]
-            index = row(("g", j % 4))
-            tile = joined(
-                _take(left_ref[md, h, j // 4], index),
-                _take(right_ref[md, h, j // 4], index),
-                _roll(a, 28 - SLOT * r),
-                _roll(b, 56 - SLOT * r),
-            )
-            if s == BLOCK:
-                a_ref[pl.ds(md * Y, Y), :] = tile
-                continue
-            sl_ref[pl.ds((md * BLOCK + s) * 16, Y), :] = tile
-            index = row(("f", j))
-            f_ref[pl.ds((md * BLOCK + s) * Y, Y), :] = 2.0 * joined(
-                f_parts(left_ref, md, h, j, index),
-                f_parts(right_ref, md, h, j, index),
-                _roll(a, -SLOT * r),
-                _roll(b, 28 - SLOT * r),
-            )
-        return 0
-
-    lax.fori_loop(0, PARTS, unpack, 0)
+    own = (lane >= 28) & (lane < 84)
+    far = (lane < 14) | (lane >= 98)
+
+    for j in range(8):
+        g_index, f_index = row(("g", j % 4)), row(("f", j))
+        for md in range(PARTS):
+            for h in range(2):
+                m = md * BLOCK + 8 * h + j
+                sides = [_take(ref[md, h, j // 4], g_index) for ref in (left_ref, right_ref)]
+                tile = jnp.where(from_left, sides[0], sides[1])
+                if 8 * h + j == BLOCK:
+                    a_ref[Y * md : Y * md + Y] = jnp.where(own, own_a_ref[md], tile)
+                else:
+                    sl_ref[16 * m : 16 * m + Y] = jnp.where(own, own_s_ref[m], tile)
+        for md in range(PARTS):
+            for h in range(2):
+                m = md * BLOCK + 8 * h + j
+                if 8 * h + j == BLOCK:
+                    continue
+                sides = []
+                for ref in (left_ref, right_ref):
+                    side = _take(ref[md, h, 2], f_index)
+                    if j >= 6:
+                        side = jnp.where(far, _take(ref[md, h, j - 6], f_index), side)
+                    sides.append(side)
+                tile = jnp.where(from_left, sides[0], sides[1])
+                f_ref[Y * m : Y * m + Y] = 2.0 * jnp.where(own, own_f_ref[m], tile)
     b_ref[pl.ds(0, TERMS * Y), :] = 6.0 * a_ref[...] + near(a_ref[...])
     inside = a_ref[pl.ds(0, Y), :] > 0.0
     scale = jnp.where(inside, 1.0 / jnp.where(inside, b_ref[pl.ds(0, Y), :], 1.0), 0.0)
@@ -277,7 +280,7 @@
             w_ref[pl.ds(i * Y, Y), :] = f_ref[pl.ds(i * Y, Y), :] - v
             return 0
 
-        lax.fori_loop(0, MODES, mix, 0, unroll=4)
+        lax.fori_loop(0, MODES, mix, 0, unroll=8)
         for first_mode in range(0, MODES, chunk):
             rows = pl.ds(first_mode * Y, chunk * Y)
             x = (w_ref[rows, :] + near(u_ref[rows, :])).reshape(chunk, Y, 128) * scale[None]
@@ -344,49 +347,60 @@
     return (low & 127) * 16 + (high & 127) * (16 << 16), c1, c2
 
 
+def _call(kernel, outs, smem, name, scratch=()):
+    def run(*args):
+        args = [
+            x if n < smem or isinstance(x, _Plain) else pltpu.with_memory_space_constraint(x, pltpu.VMEM)
+            for n, x in enumerate(args)
+        ]
+        return pl.pallas_call(
+            kernel,
+            out_shape=outs,
+            in_specs=_smem(smem) + _vmem(len(args) - smem),
+            out_specs=_vmem(len(outs)),
+            scratch_shapes=scratch,
+            name=name,
+        )(*[x.value if isinstance(x, _Plain) else x for x in args])
+
+    return run
+
+
+class _Plain:
+    def __init__(self, value):
+        self.value = value
+
+
 def per_device(guess, source, mean_coef, fluct_coef, triples, coupling):
     tile = (Y, 128)
-    table = jnp.asarray(TABLE)
+    table = _Plain(jnp.asarray(TABLE))
+    near = _Plain(jnp.asarray(NEAR, jnp.bfloat16))
     which = lax.axis_index("mode").astype(jnp.int32).reshape(1)
-    message = pl.pallas_call(
-        _send_kernel,
-        out_shape=jax.ShapeDtypeStruct((GROUP, PARTS) + tile, F32),
-        in_specs=_smem(1) + _vmem(4),
-        out_specs=_vmem(1)[0],
-        name="send",
-    )(which, guess, source, mean_coef, fluct_coef)
+
+    def kept(*shape):
+        return pltpu.VMEM(shape + tile, F32)
+
+    given = [_Plain(x) for x in (guess, source, mean_coef, fluct_coef)]
+    (message,) = _call(_send_kernel, [kept(GROUP, PARTS)], 1, "send")(which, *given)
     block = lax.all_to_all(message, ("slab", "mode"), 0, 0, tiled=True)
-    to_right, to_left = pl.pallas_call(
-        _halo_kernel,
-        out_shape=[jax.ShapeDtypeStruct((PARTS, 2, 3) + tile, F32)] * 2,
-        in_specs=_vmem(2),
-        out_specs=_vmem(2),
-        name="halo",
-    )(table, block)
     count = lax.axis_size("pair")
+    halo = [kept(PARTS, 2, 3)]
+    (to_right,) = _call(functools.partial(_halo_kernel, "right"), halo, 0, "halo_right")(table, block)
     from_left = lax.ppermute(to_right, "pair", [(n, n + 1) for n in range(count - 1)])
+    (to_left,) = _call(functools.partial(_halo_kernel, "left"), halo, 0, "halo_left")(table, block)
     from_right = lax.ppermute(to_left, "pair", [(n + 1, n) for n in range(count - 1)])
+    own = _call(_own_kernel, [kept(MODES), kept(MODES), kept(TERMS)], 0, "own")(block)
     jj, c1, c2 = pattern_tables(triples, coupling)
-    result = pl.pallas_call(
-        _sweep_kernel,
-        out_shape=jax.ShapeDtypeStruct((GROUP, 4) + tile, F32),
-        in_specs=_smem(3) + _vmem(5),
-        out_specs=_vmem(1)[0],
-        scratch_shapes=[pltpu.VMEM((MODES * 16, 128), F32)]
+    scratch = (
+        [pltpu.VMEM((MODES * 16, 128), F32)]
         + [pltpu.VMEM((MODES * Y, 128), F32)] * 4
-        + [pltpu.VMEM((TERMS * Y, 128), F32)] * 2,
-        name="sweeps",
-    )(jj, c1, c2, table, jnp.asarray(NEAR, jnp.bfloat16), block, from_left, from_right)
+        + [pltpu.VMEM((TERMS * Y, 128), F32)] * 2
+    )
+    (result,) = _call(_sweep_kernel, [kept(GROUP, 4)], 3, "sweeps", scratch)(
+        jj, c1, c2, table, near, *own, from_left, from_right
+    )
     pieces = lax.all_to_all(result, ("slab", "mode"), 0, 0, tiled=True)
-    return tuple(
-        pl.pallas_call(
-            _receive_kernel,
-            out_shape=[jax.ShapeDtypeStruct(guess.shape, F32)] * 2,
-            in_specs=_vmem(1),
-            out_specs=_vmem(2),
-            name="receive",
-        )(pieces)
-    )
+    outs = [jax.ShapeDtypeStruct(guess.shape, F32)] * 2
+    return tuple(_call(_receive_kernel, outs, 0, "receive")(pieces))
 
 
 def solution(mesh):

time: 75.7 us -> 67 us (0.89)
  Pallas kernels: 23.6 us -> 17.6 us
  local copies, waits for them, and re-layouts: 1.47 us -> 0.01 us
    pallas_call x4 -> x6, Pallas kernels: 23.6 us -> 17.6 us  [run(): pl.pallas_call(kernel, out_shape=outs, in_specs=_smem(smem) + _vmem(len(a...]
    ppermute x1, waiting for transfers between devices: 2.17 us -> 0.4 us  [per_device(): lax.ppermute(to_right, 'pair', [(n, n + 1) for n in range(count - 1)])]
    unnamed x10 -> x4, local copies, waits for them, and re-layouts: 1.47 us -> 0.01 us
    ppermute x1, waiting for transfers between devices: 4.19 us -> 5.22 us  [per_device(): lax.ppermute(to_left, 'pair', [(n + 1, n) for n in range(count - 1)])]
  transfers between devices with their start and end apart: 3 -> 3, of which waited for: 3 -> 3; matrix products, arithmetic and copies ran while one was open for 6% -> 7% of each run, Pallas kernels for 0% -> 2%
where the time goes in v3:
time: 67 us; the launch traced here: 66.5 us
  starting transfers between devices  18.9 us (28%)
  Pallas kernels  17.6 us (26%)
  waiting for transfers between devices  12.6 us (19%)
  blocking collectives  12.2 us (18%)
  other arithmetic  4.41 us (7%)
  between operations  0.73 us (1%)
    pallas_call x6, Pallas kernels, run(): pl.pallas_call(kernel, out_shape=outs, in_specs=_smem(smem) + _vmem(len(a...  17.6 us
    all_to_all x1, blocking collectives, per_device(): pieces = lax.all_to_all(result, ('slab', 'mode'), 0, 0, tiled=True)  12.2 us
    ppermute x1, starting transfers between devices, per_device(): lax.ppermute(to_left, 'pair', [(n + 1, n) for n in range(count - 1)])  7.87 us
    all_to_all x1, waiting for transfers between devices, per_device(): block = lax.all_to_all(message, ('slab', 'mode'), 0, 0, tiled=True)  6.97 us
    all_to_all x1, starting transfers between devices, per_device(): block = lax.all_to_all(message, ('slab', 'mode'), 0, 0, tiled=True)  5.89 us
    ppermute x1, waiting for transfers between devices, per_device(): lax.ppermute(to_left, 'pair', [(n + 1, n) for n in range(count - 1)])  5.22 us
    ppermute x1, starting transfers between devices, per_device(): lax.ppermute(to_right, 'pair', [(n, n + 1) for n in range(count - 1)])  5.18 us
    reduce_sum x1, other arithmetic, pattern_tables(): jnp.sum(jnp.where(code[:, None] == high[None, :], coupling[:, None], 0.0)...  2.02 us
  transfers between devices with their start and end apart: 3, of which 3 were waited for; matrix products, arithmetic and copies ran while one was open for 7% of the time, Pallas kernels for 2%

profile of v3, /device:TPU:24, one launch (start us, length us, event | category | flops | bytes accessed | tf_op | source)
XLA Modules:
  0.0 66.5 jit_solution(10030822802253576332)
XLA Ops:
  0.6 2.3 %send.1 = f32[16,8,8,128]{3,2,1,0:T(8,128)} custom-call(s32[1]{0:T(128)} %bitcast.which_ref, f32[15,2,8,128]{3,2,1,0:T(8,128)} %guess_ref.1, f32[15,2,8,128]{3,2,1,0:T(8,128)} %source_ref.1, f32[2,8,128]{2,1,0:T(8,128)} %mean_ref.1, f32[7,2,8,128]{3,2,1,0:T(8,128)} %fluct_ref.1), custom_call_target="tpu_custom_call" | custom-call | tf_op jit(solution)/shard_map/send/pallas_call | solution.py:356
  3.0 0.0 copy-start
  3.0 0.0 copy-start.1
  3.0 5.9 %all-to-all-start = ((f32[16,8,8,128]{3,2,1,0:T(8,128)}), f32[16,8,8,128]{3,2,1,0:T(8,128)S(1)}, u32[]{:S(2)}, u32[]{:S(2)}) async-start(f32[16,8,8,128]{3,2,1,0:T(8,128)} %send.1), calls=%async_computation | async-start | bytes 1048576 | tf_op jit(solution)/shard_map/all_to_all | solution.py:384
  8.9 0.0 copy-done
  8.9 0.1 slice_reduce_fusion
  9.0 1.7 %select_reduce_fusion.3 = (s32[840]{0:T(1024)S(1)}, s32[840]{0:T(1024)S(1)}) fusion(s32[1680]{0:T(1024)S(1)} %get-tuple-element.9, s32[1680]{0:T(1024)S(1)} %multiply_add_fusion), kind=kLoop, calls=%fused_computation.3 | loop fusion | flops 7054320 | bytes 20160 | tf_op jit(solution)/shard_map/reduce_min | solution.py:343
  10.7 0.0 copy-done.1
  10.7 2.0 %select_reduce_fusion = (f32[840]{0:T(1024)}, f32[840]{0:T(1024)}) fusion(s32[840]{0:T(1024)S(1)} %get-tuple-element.13, f32[1680]{0:T(1024)S(1)} %copy-done.1, s32[1680]{0:T(1024)S(1)} %multiply_add_fusion, s32[840]{0:T(1024)S(1)} %get-tuple-element.12), kind=kLoop, calls=%fused_computation | loop fusion | flops 8465520 | bytes 26880 | tf_op jit(solution)/shard_map/reduce_sum | solution.py:346
  12.7 7.0 %all-to-all-done.block_ref = f32[16,8,8,128]{3,2,1,0:T(8,128)S(1)} async-done(((f32[16,8,8,128]{3,2,1,0:T(8,128)}), f32[16,8,8,128]{3,2,1,0:T(8,128)S(1)}, u32[]{:S(2)}, u32[]{:S(2)}) %all-to-all-start) | async-done | bytes 524320 | tf_op jit(solution)/shard_map/all_to_all | solution.py:384
  19.7 1.0 %halo_right.1 = f32[8,2,3,8,128]{4,3,2,1,0:T(8,128)S(1)} custom-call(s32[32,128]{1,0:T(8,128)} %constant.30.clone.table_ref, f32[16,8,8,128]{3,2,1,0:T(8,128)S(1)} %all-to-all-done.block_ref), custom_call_target="tpu_custom_call" | custom-call | tf_op jit(solution)/shard_map/halo_right/pallas_call | solution.py:356
  20.7 5.2 %collective-permute-start = (f32[8,2,3,8,128]{4,3,2,1,0:T(8,128)S(1)}, f32[8,2,3,8,128]{4,3,2,1,0:T(8,128)S(1)}, u32[]{:S(2)}, u32[]{:S(2)}) collective-permute-start(f32[8,2,3,8,128]{4,3,2,1,0:T(8,128)S(1)} %halo_right.1), channel_id=1, source_target_pairs={{0,16},{16,32},{32,48},{48,64},{64,80},{80,96},{96,112},{112,128},... | collective-permute-start | bytes 589832 | tf_op jit(solution)/shard_map/ppermute | solution.py:388
  25.9 1.0 %halo_left.1 = f32[8,2,3,8,128]{4,3,2,1,0:T(8,128)S(1)} custom-call(s32[32,128]{1,0:T(8,128)} %constant.30.clone.table_ref, f32[16,8,8,128]{3,2,1,0:T(8,128)S(1)} %all-to-all-done.block_ref), custom_call_target="tpu_custom_call" | custom-call | tf_op jit(solution)/shard_map/halo_left/pallas_call | solution.py:356
  26.9 7.9 %collective-permute-start.1 = (f32[8,2,3,8,128]{4,3,2,1,0:T(8,128)S(1)}, f32[8,2,3,8,128]{4,3,2,1,0:T(8,128)S(1)}, u32[]{:S(2)}, u32[]{:S(2)}) collective-permute-start(f32[8,2,3,8,128]{4,3,2,1,0:T(8,128)S(1)} %halo_left.1), channel_id=1, source_target_pairs={{16,0},{32,16},{48,32},{64,48},{80,64},{96,80},{112,96},{128,112},... | collective-permute-start | bytes 589832 | tf_op jit(solution)/shard_map/ppermute | solution.py:390
  34.8 0.6 multiply_add_fusion.1.jj_ref
  35.4 0.5 own.1
  35.9 0.4 collective-permute-done.left_ref
  36.3 5.2 %collective-permute-done.1.right_ref = f32[8,2,3,8,128]{4,3,2,1,0:T(8,128)S(1)} collective-permute-done((f32[8,2,3,8,128]{4,3,2,1,0:T(8,128)S(1)}, f32[8,2,3,8,128]{4,3,2,1,0:T(8,128)S(1)}, u32[]{:S(2)}, u32[]{:S(2)}) %collective-permute-start.1) | collective-permute-done | bytes 196640 | tf_op jit(solution)/shard_map/ppermute | solution.py:390
  41.6 11.7 %sweeps.1 = f32[16,4,8,128]{3,2,1,0:T(8,128)S(1)} custom-call(s32[840]{0:T(1024)} %multiply_add_fusion.1.jj_ref, f32[840]{0:T(1024)} %get-tuple-element.11.c1_ref, f32[840]{0:T(1024)} %get-tuple-element.10.c2_ref, s32[32,128]{1,0:T(8,128)} %constant.30.clone.table_ref, bf16[384,128]{1,0:T(8,128)(2,1)} %constant.31.clone.near_ref, ...), custom_call_target="tpu_custom_call" | custom-call | tf_op jit(solution)/shard_map/sweeps/pallas_call | solution.py:356
  53.2 12.2 %all_to_all.10.piece_ref = f32[16,4,8,128]{3,2,1,0:T(8,128)S(1)} all-to-all(f32[16,4,8,128]{3,2,1,0:T(8,128)S(1)} %sweeps.1), channel_id=1, replica_groups=mesh['pair'=32,'slab'=2,'mode'=8] {'slab','mode'}, dimensions={0} | all-to-all | bytes 524288 | tf_op jit(solution)/shard_map/all_to_all | solution.py:401
  65.5 1.1 %receive.1 = (f32[15,2,8,128]{3,2,1,0:T(8,128)}, f32[15,2,8,128]{3,2,1,0:T(8,128)}) custom-call(f32[16,4,8,128]{3,2,1,0:T(8,128)S(1)} %all_to_all.10.piece_ref), custom_call_target="tpu_custom_call" | custom-call | tf_op jit(solution)/shard_map/receive/pallas_call | solution.py:356
  (1 shorter events, 0.0 us)
Async XLA Ops:
  3.0 5.9 %copy-start = (s32[3,1680]{1,0:T(4,128)S(1)}, s32[3,1680]{1,0:T(4,128)}, u32[]{:S(2)}) copy-start(s32[3,1680]{1,0:T(4,128)} %param.12) | copy-start | bytes 60484
  3.0 7.7 %copy-start.1 = (f32[1680]{0:T(1024)S(1)}, f32[1680]{0:T(1024)}, u32[]{:S(2)}) copy-start(f32[1680]{0:T(1024)} %param.13) | copy-start | bytes 20164
  3.0 16.7 %all-to-all-start = ((f32[16,8,8,128]{3,2,1,0:T(8,128)}), f32[16,8,8,128]{3,2,1,0:T(8,128)S(1)}, u32[]{:S(2)}, u32[]{:S(2)}) async-start(f32[16,8,8,128]{3,2,1,0:T(8,128)} %send.1), calls=%async_computation | async-start | bytes 1048576 | tf_op jit(solution)/shard_map/all_to_all | solution.py:384
  20.7 15.6 %collective-permute-start = (f32[8,2,3,8,128]{4,3,2,1,0:T(8,128)S(1)}, f32[8,2,3,8,128]{4,3,2,1,0:T(8,128)S(1)}, u32[]{:S(2)}, u32[]{:S(2)}) collective-permute-start(f32[8,2,3,8,128]{4,3,2,1,0:T(8,128)S(1)} %halo_right.1), channel_id=1, source_target_pairs={{0,16},{16,32},{32,48},{48,64},{64,80},{80,96},{96,112},{112,128},... | collective-permute-start | bytes 589832 | tf_op jit(solution)/shard_map/ppermute | solution.py:388
  26.9 14.6 %collective-permute-start.1 = (f32[8,2,3,8,128]{4,3,2,1,0:T(8,128)S(1)}, f32[8,2,3,8,128]{4,3,2,1,0:T(8,128)S(1)}, u32[]{:S(2)}, u32[]{:S(2)}) collective-permute-start(f32[8,2,3,8,128]{4,3,2,1,0:T(8,128)S(1)} %halo_left.1), channel_id=1, source_target_pairs={{16,0},{32,16},{48,32},{64,48},{80,64},{96,80},{112,96},{128,112},... | collective-permute-start | bytes 589832 | tf_op jit(solution)/shard_map/ppermute | solution.py:390

commit v4 on v3

--- a/solution.py
+++ b/solution.py
@@ -17,6 +17,7 @@
 MODES = 120
 TERMS = 8
 Y, Z = 8, 128
+STEP = 8
 ZW = 8
 PW = 14
 SLOT = 64
@@ -196,8 +197,19 @@
             f_ref[md * BLOCK + s] = jnp.where(first, _roll(a, -SLOT * r), _roll(b, 28 - SLOT * r))
 
 
+def _values_kernel(c1_ref, c2_ref, out_ref):
+    def body(n, _):
+        for r in range(8):
+            at = 8 * n + r
+            out_ref[pl.ds(2 * at, 1), :] = jnp.full((1, 128), c1_ref[at])
+            out_ref[pl.ds(2 * at + 1, 1), :] = jnp.full((1, 128), c2_ref[at])
+        return 0
+
+    lax.fori_loop(0, MODES * (TERMS - 1) // 8, body, 0)
+
+
 def _sweep_kernel(
-    jj_ref, c1_ref, c2_ref, table_ref, near_ref, own_s_ref, own_f_ref, own_a_ref, left_ref, right_ref,
+    j1_ref, j2_ref, value_ref, table_ref, near_ref, own_s_ref, own_f_ref, own_a_ref, left_ref, right_ref,
     out_ref, sl_ref, u_ref, w_ref, f_ref, up_ref, a_ref, b_ref,
 ):
     lane = _lane()
@@ -207,6 +219,9 @@
 
     def row(name):
         return jnp.broadcast_to(table_ref[pl.ds(AT[name], 1), :], (Y, 128))
+
+    def value(at):
+        return jnp.broadcast_to(value_ref[pl.ds(at, 1), :], (Y, 128))
 
     def near(x):
         high = x.astype(jnp.bfloat16)
@@ -261,26 +276,31 @@
             for n in range(chunk):
                 sl_ref[16 * (first_mode + n) + Y : 16 * (first_mode + n) + 16] = x[Y * n : Y * n + Y]
 
-        def mix(i, _):
-            mine = sl_ref[pl.ds(i * 16, Y), :]
+        def mix(n, _):
+            first_i = n * STEP
+            modes = [first_i + r for r in range(STEP)]
             a, b = a_ref[0:Y], b_ref[0:Y]
-            u = a * mine
-            v = b * mine - a * sl_ref[pl.ds(i * 16 + Y, Y), :]
+            us, ws = [], []
+            for i in modes:
+                mine = sl_ref[pl.ds(i * 16, Y), :]
+                us.append(a * mine)
+                ws.append(f_ref[pl.ds(i * Y, Y), :] - (b * mine - a * sl_ref[pl.ds(i * 16 + Y, Y), :]))
             for k in range(1, TERMS):
-                at = i * (TERMS - 1) + (k - 1)
-                jj, c1, c2 = jj_ref[at], c1_ref[at], c2_ref[at]
-                j1 = pl.multiple_of(jj & 0xFFFF, 16)
-                j2 = pl.multiple_of(jj >> 16, 16)
-                m = c1 * sl_ref[pl.ds(j1, Y), :] + c2 * sl_ref[pl.ds(j2, Y), :]
-                lm = c1 * sl_ref[pl.ds(j1 + Y, Y), :] + c2 * sl_ref[pl.ds(j2 + Y, Y), :]
                 a, b = a_ref[Y * k : Y * k + Y], b_ref[Y * k : Y * k + Y]
-                u = u + a * m
-                v = v + (b * m - a * lm)
-            u_ref[pl.ds(i * Y, Y), :] = u
-            w_ref[pl.ds(i * Y, Y), :] = f_ref[pl.ds(i * Y, Y), :] - v
+                for r, i in enumerate(modes):
+                    at = first_i * (TERMS - 1) + (r * (TERMS - 1) + k - 1)
+                    j1, j2 = pl.multiple_of(j1_ref[at], 16), pl.multiple_of(j2_ref[at], 16)
+                    c1, c2 = value(2 * at), value(2 * at + 1)
+                    m = c1 * sl_ref[pl.ds(j1, Y), :] + c2 * sl_ref[pl.ds(j2, Y), :]
+                    lm = c1 * sl_ref[pl.ds(j1 + Y, Y), :] + c2 * sl_ref[pl.ds(j2 + Y, Y), :]
+                    us[r] = us[r] + a * m
+                    ws[r] = ws[r] - (b * m - a * lm)
+            for r, i in enumerate(modes):
+                u_ref[pl.ds(i * Y, Y), :] = us[r]
+                w_ref[pl.ds(i * Y, Y), :] = ws[r]
             return 0
 
-        lax.fori_loop(0, MODES, mix, 0, unroll=8)
+        lax.fori_loop(0, MODES // STEP, mix, 0)
         for first_mode in range(0, MODES, chunk):
             rows = pl.ds(first_mode * Y, chunk * Y)
             x = (w_ref[rows, :] + near(u_ref[rows, :])).reshape(chunk, Y, 128) * scale[None]
@@ -293,22 +313,23 @@
     lax.fori_loop(0, ITERS, sweep, 0)
     home = (lane >= 28) & (lane < 84)
 
-    def pack(md, _):
-        both = []
-        for m in range(BLOCK):
-            i = md * BLOCK + m
-            both.append(jnp.where(home, sl_ref[pl.ds(i * 16, Y), :], _roll(up_ref[pl.ds(i * Y, Y), :], 64)))
-        for slab in range(SLABS):
-            index = row(("own", slab))
+    for slab in range(SLABS):
+        index = row(("own", slab))
+        for md in range(PARTS):
             for t in range(4):
-                tile = _take(both[4 * t], index)
-                for r in range(1, 4):
-                    if 4 * t + r < BLOCK:
-                        tile = jnp.where(lane >= 32 * r, _take(both[4 * t + r], index), tile)
+                tile = None
+                for r in range(4):
+                    i = md * BLOCK + 4 * t + r
+                    if 4 * t + r == BLOCK:
+                        continue
+                    if slab == 0:
+                        both = jnp.where(home, sl_ref[16 * i : 16 * i + Y], _roll(up_ref[Y * i : Y * i + Y], 64))
+                        u_ref[Y * i : Y * i + Y] = both
+                    else:
+                        both = u_ref[Y * i : Y * i + Y]
+                    both = _take(both, index)
+                    tile = both if r == 0 else jnp.where(lane >= 32 * r, both, tile)
                 out_ref[slab * PARTS + md, t] = tile
-        return 0
-
-    lax.fori_loop(0, PARTS, pack, 0)
 
 
 def _receive_kernel(piece_ref, solution_ref, update_ref):
@@ -344,7 +365,7 @@
     high = jnp.max(jnp.where(match, code[:, None], -1), axis=0)
     c1 = jnp.sum(jnp.where(code[:, None] == low[None, :], coupling[:, None], 0.0), axis=0)
     c2 = jnp.sum(jnp.where(code[:, None] == high[None, :], coupling[:, None], 0.0), axis=0)
-    return (low & 127) * 16 + (high & 127) * (16 << 16), c1, c2
+    return (low & 127) * 16, (high & 127) * 16, c1, c2
 
 
 def _call(kernel, outs, smem, name, scratch=()):
@@ -389,14 +410,16 @@
     (to_left,) = _call(functools.partial(_halo_kernel, "left"), halo, 0, "halo_left")(table, block)
     from_right = lax.ppermute(to_left, "pair", [(n + 1, n) for n in range(count - 1)])
     own = _call(_own_kernel, [kept(MODES), kept(MODES), kept(TERMS)], 0, "own")(block)
-    jj, c1, c2 = pattern_tables(triples, coupling)
+    triples, coupling, _ = lax.optimization_barrier((triples, coupling, to_right))
+    j1, j2, c1, c2 = pattern_tables(triples, coupling)
+    (values,) = _call(_values_kernel, [pltpu.VMEM((2 * MODES * (TERMS - 1), 128), F32)], 2, "values")(c1, c2)
     scratch = (
         [pltpu.VMEM((MODES * 16, 128), F32)]
         + [pltpu.VMEM((MODES * Y, 128), F32)] * 4
         + [pltpu.VMEM((TERMS * Y, 128), F32)] * 2
     )
-    (result,) = _call(_sweep_kernel, [kept(GROUP, 4)], 3, "sweeps", scratch)(
-        jj, c1, c2, table, near, *own, from_left, from_right
+    (result,) = _call(_sweep_kernel, [kept(GROUP, 4)], 2, "sweeps", scratch)(
+        j1, j2, values, table, near, *own, from_left, from_right
     )
     pieces = lax.all_to_all(result, ("slab", "mode"), 0, 0, tiled=True)
     outs = [jax.ShapeDtypeStruct(guess.shape, F32)] * 2

time: 67 us -> 64.1 us (0.957)
  blocking collectives: 12.2 us -> 28.3 us
  waiting for transfers between devices: 12.6 us -> 0.01 us
  starting transfers between devices: 18.9 us -> 13 us
    all_to_all x0 -> x1, blocking collectives: none -> 16.4 us  [per_device(): block = lax.all_to_all(message, ('slab', 'mode'), 0, 0, tiled=True)]
    all_to_all x1 -> x0, waiting for transfers between devices: 6.97 us -> none  [per_device(): block = lax.all_to_all(message, ('slab', 'mode'), 0, 0, tiled=True)]
    all_to_all x1 -> x0, starting transfers between devices: 5.89 us -> none  [per_device(): block = lax.all_to_all(message, ('slab', 'mode'), 0, 0, tiled=True)]
    ppermute x1, waiting for transfers between devices: 5.22 us -> 0.01 us  [per_device(): lax.ppermute(to_left, 'pair', [(n + 1, n) for n in range(count - 1)])]
    reduce_max x0 -> x1, other arithmetic: none -> 1.74 us  [pattern_tables(): high = jnp.max(jnp.where(match, code[:, None], -1), axis=0)]
    reduce_min x1 -> x0, other arithmetic: 1.74 us -> none  [pattern_tables(): low = jnp.min(jnp.where(match, code[:, None], entries * 128), axis=0)]
    pallas_call x6 -> x7, Pallas kernels: 17.6 us -> 17.1 us  [run(): pl.pallas_call(kernel, out_shape=outs, in_specs=_smem(smem) + _vmem(len(a...]
  transfers between devices with their start and end apart: 3 -> 2, of which waited for: 3 -> 0; matrix products, arithmetic and copies ran while one was open for 7% -> 7% of each run, Pallas kernels for 2% -> 6%
where the time goes in v4:
time: 64.1 us; the launch traced here: 63.6 us
  blocking collectives  28.3 us (44%)
  Pallas kernels  17.1 us (27%)
  starting transfers between devices  13 us (20%)
  other arithmetic  4.41 us (7%)
  between operations  0.74 us (1%)
    pallas_call x7, Pallas kernels, run(): pl.pallas_call(kernel, out_shape=outs, in_specs=_smem(smem) + _vmem(len(a...  17.1 us
    all_to_all x1, blocking collectives, per_device(): block = lax.all_to_all(message, ('slab', 'mode'), 0, 0, tiled=True)  16.4 us
    all_to_all x1, blocking collectives, per_device(): pieces = lax.all_to_all(result, ('slab', 'mode'), 0, 0, tiled=True)  12 us
    ppermute x1, starting transfers between devices, per_device(): lax.ppermute(to_left, 'pair', [(n + 1, n) for n in range(count - 1)])  7.87 us
    ppermute x1, starting transfers between devices, per_device(): lax.ppermute(to_right, 'pair', [(n, n + 1) for n in range(count - 1)])  5.18 us
    reduce_sum x1, other arithmetic, pattern_tables(): jnp.sum(jnp.where(code[:, None] == high[None, :], coupling[:, None], 0.0)...  2.02 us
    reduce_max x1, other arithmetic, pattern_tables(): high = jnp.max(jnp.where(match, code[:, None], -1), axis=0)  1.74 us
  transfers between devices with their start and end apart: 2, of which 0 were waited for; matrix products, arithmetic and copies ran while one was open for 7% of the time, Pallas kernels for 6%

profile of v4, /device:TPU:24, one launch (start us, length us, event | category | flops | bytes accessed | tf_op | source)
XLA Modules:
  0.0 63.6 jit_solution(4794365641218037215)
XLA Ops:
  0.6 1.5 %send.1 = f32[16,8,8,128]{3,2,1,0:T(8,128)S(1)} custom-call(s32[1]{0:T(128)} %bitcast.which_ref, f32[15,2,8,128]{3,2,1,0:T(8,128)} %guess_ref.1, f32[15,2,8,128]{3,2,1,0:T(8,128)} %source_ref.1, f32[2,8,128]{2,1,0:T(8,128)} %mean_ref.1, f32[7,2,8,128]{3,2,1,0:T(8,128)} %fluct_ref.1), custom_call_target="tpu_custom_call" | custom-call | tf_op jit(solution)/shard_map/send/pallas_call | solution.py:377
  2.2 0.0 copy-start
  2.2 16.4 %all_to_all.10.block_ref = f32[16,8,8,128]{3,2,1,0:T(8,128)S(1)} all-to-all(f32[16,8,8,128]{3,2,1,0:T(8,128)S(1)} %send.1), channel_id=1, replica_groups=mesh['pair'=32,'slab'=2,'mode'=8] {'slab','mode'}, dimensions={0} | all-to-all | bytes 1048576 | tf_op jit(solution)/shard_map/all_to_all | solution.py:405
  18.6 0.0 copy-start.1
  18.6 1.0 %halo_right.1 = f32[8,2,3,8,128]{4,3,2,1,0:T(8,128)S(1)} custom-call(s32[32,128]{1,0:T(8,128)} %constant.28.clone.table_ref, f32[16,8,8,128]{3,2,1,0:T(8,128)S(1)} %all_to_all.10.block_ref), custom_call_target="tpu_custom_call" | custom-call | tf_op jit(solution)/shard_map/halo_right/pallas_call | solution.py:377
  19.6 5.2 %collective-permute-start = (f32[8,2,3,8,128]{4,3,2,1,0:T(8,128)S(1)}, f32[8,2,3,8,128]{4,3,2,1,0:T(8,128)S(1)}, u32[]{:S(2)}, u32[]{:S(2)}) collective-permute-start(f32[8,2,3,8,128]{4,3,2,1,0:T(8,128)S(1)} %halo_right.1), channel_id=1, source_target_pairs={{0,16},{16,32},{32,48},{48,64},{64,80},{80,96},{96,112},{112,128},... | collective-permute-start | bytes 589832 | tf_op jit(solution)/shard_map/ppermute | solution.py:409
  24.8 0.0 copy-done
  24.8 0.1 slice_reduce_fusion
  24.9 1.0 %halo_left.1 = f32[8,2,3,8,128]{4,3,2,1,0:T(8,128)S(1)} custom-call(s32[32,128]{1,0:T(8,128)} %constant.28.clone.table_ref, f32[16,8,8,128]{3,2,1,0:T(8,128)S(1)} %all_to_all.10.block_ref), custom_call_target="tpu_custom_call" | custom-call | tf_op jit(solution)/shard_map/halo_left/pallas_call | solution.py:377
  25.9 7.9 %collective-permute-start.1 = (f32[8,2,3,8,128]{4,3,2,1,0:T(8,128)S(1)}, f32[8,2,3,8,128]{4,3,2,1,0:T(8,128)S(1)}, u32[]{:S(2)}, u32[]{:S(2)}) collective-permute-start(f32[8,2,3,8,128]{4,3,2,1,0:T(8,128)S(1)} %halo_left.1), channel_id=1, source_target_pairs={{16,0},{32,16},{48,32},{64,48},{80,64},{96,80},{112,96},{128,112},... | collective-permute-start | bytes 589832 | tf_op jit(solution)/shard_map/ppermute | solution.py:411
  33.8 1.7 %select_reduce_fusion.2 = (s32[840]{0:T(1024)S(1)}, s32[840]{0:T(1024)S(1)}) fusion(s32[1680]{0:T(1024)S(1)} %get-tuple-element.13, s32[1680]{0:T(1024)S(1)} %multiply_add_fusion), kind=kLoop, calls=%fused_computation.2 | loop fusion | flops 7054320 | bytes 20160 | tf_op jit(solution)/shard_map/reduce_max | solution.py:365
  35.5 0.0 copy-done.1
  35.6 2.0 %select_reduce_fusion = (f32[840]{0:T(1024)}, f32[840]{0:T(1024)}) fusion(s32[840]{0:T(1024)S(1)} %get-tuple-element.16, f32[1680]{0:T(1024)S(1)} %copy-done.1, s32[1680]{0:T(1024)S(1)} %multiply_add_fusion, s32[840]{0:T(1024)S(1)} %get-tuple-element.17), kind=kLoop, calls=%fused_computation | loop fusion | flops 8465520 | bytes 26880 | tf_op jit(solution)/shard_map/reduce_sum | solution.py:367
  37.6 2.1 %values.1.value_ref = f32[1680,128]{1,0:T(8,128)S(1)} custom-call(f32[840]{0:T(1024)} %get-tuple-element.15.c1_ref, f32[840]{0:T(1024)} %get-tuple-element.14.c2_ref), custom_call_target="tpu_custom_call" | custom-call | tf_op jit(solution)/shard_map/values/pallas_call | solution.py:377
  39.7 0.5 own.1
  40.2 0.6 and_multiply_fusion
  40.8 0.0 collective-permute-done.1.right_ref
  40.8 0.0 collective-permute-done.left_ref
  40.8 9.8 %sweeps.1 = f32[16,4,8,128]{3,2,1,0:T(8,128)S(1)} custom-call(s32[840]{0:T(1024)} %get-tuple-element.19.j1_ref, s32[840]{0:T(1024)} %get-tuple-element.18.j2_ref, f32[1680,128]{1,0:T(8,128)S(1)} %values.1.value_ref, s32[32,128]{1,0:T(8,128)} %constant.28.clone.table_ref, bf16[384,128]{1,0:T(8,128)(2,1)} %constant.29.clone.near_ref, ...), custom_call_target="tpu_custom_call" | custom-call | tf_op jit(solution)/shard_map/sweeps/pallas_call | solution.py:377
  50.6 12.0 %all_to_all.11.piece_ref = f32[16,4,8,128]{3,2,1,0:T(8,128)S(1)} all-to-all(f32[16,4,8,128]{3,2,1,0:T(8,128)S(1)} %sweeps.1), channel_id=1, replica_groups=mesh['pair'=32,'slab'=2,'mode'=8] {'slab','mode'}, dimensions={0} | all-to-all | bytes 524288 | tf_op jit(solution)/shard_map/all_to_all | solution.py:424
  62.6 1.1 %receive.1 = (f32[15,2,8,128]{3,2,1,0:T(8,128)}, f32[15,2,8,128]{3,2,1,0:T(8,128)}) custom-call(f32[16,4,8,128]{3,2,1,0:T(8,128)S(1)} %all_to_all.11.piece_ref), custom_call_target="tpu_custom_call" | custom-call | tf_op jit(solution)/shard_map/receive/pallas_call | solution.py:377
  (1 shorter events, 0.0 us)
Async XLA Ops:
  2.2 22.6 %copy-start = (s32[3,1680]{1,0:T(4,128)S(1)}, s32[3,1680]{1,0:T(4,128)}, u32[]{:S(2)}) copy-start(s32[3,1680]{1,0:T(4,128)} %param.12) | copy-start | bytes 60484
  18.6 17.0 %copy-start.1 = (f32[1680]{0:T(1024)S(1)}, f32[1680]{0:T(1024)}, u32[]{:S(2)}) copy-start(f32[1680]{0:T(1024)} %param.13) | copy-start | bytes 20164
  19.6 21.2 %collective-permute-start = (f32[8,2,3,8,128]{4,3,2,1,0:T(8,128)S(1)}, f32[8,2,3,8,128]{4,3,2,1,0:T(8,128)S(1)}, u32[]{:S(2)}, u32[]{:S(2)}) collective-permute-start(f32[8,2,3,8,128]{4,3,2,1,0:T(8,128)S(1)} %halo_right.1), channel_id=1, source_target_pairs={{0,16},{16,32},{32,48},{48,64},{64,80},{80,96},{96,112},{112,128},... | collective-permute-start | bytes 589832 | tf_op jit(solution)/shard_map/ppermute | solution.py:409
  25.9 14.9 %collective-permute-start.1 = (f32[8,2,3,8,128]{4,3,2,1,0:T(8,128)S(1)}, f32[8,2,3,8,128]{4,3,2,1,0:T(8,128)S(1)}, u32[]{:S(2)}, u32[]{:S(2)}) collective-permute-start(f32[8,2,3,8,128]{4,3,2,1,0:T(8,128)S(1)} %halo_left.1), channel_id=1, source_target_pairs={{16,0},{32,16},{48,32},{64,48},{80,64},{96,80},{112,96},{128,112},... | collective-permute-start | bytes 589832 | tf_op jit(solution)/shard_map/ppermute | solution.py:411

commit v5 on v4

--- a/solution.py
+++ b/solution.py
@@ -380,6 +380,7 @@
             in_specs=_smem(smem) + _vmem(len(args) - smem),
             out_specs=_vmem(len(outs)),
             scratch_shapes=scratch,
+            compiler_params=None if name == "send" else pltpu.CompilerParams(vmem_limit_bytes=24 << 20),
             name=name,
         )(*[x.value if isinstance(x, _Plain) else x for x in args])
 
@@ -393,7 +394,7 @@
 
 def per_device(guess, source, mean_coef, fluct_coef, triples, coupling):
     tile = (Y, 128)
-    table = _Plain(jnp.asarray(TABLE))
+    table = jnp.asarray(TABLE)
     near = _Plain(jnp.asarray(NEAR, jnp.bfloat16))
     which = lax.axis_index("mode").astype(jnp.int32).reshape(1)
 

time: 64.1 us -> 62.5 us (0.975)
  Pallas kernels: 17.1 us -> 15.3 us
  other arithmetic: 4.41 us -> 3.23 us
  waiting for transfers between devices: 0.01 us -> 1.04 us
    pallas_call x7, Pallas kernels: 17.1 us -> 15.3 us  [run(): pl.pallas_call(kernel, out_shape=outs, in_specs=_smem(smem) + _vmem(len(a...]
    ppermute x1, waiting for transfers between devices: 0.01 us -> 1.04 us  [per_device(): lax.ppermute(to_left, 'pair', [(n + 1, n) for n in range(count - 1)])]
  transfers between devices with their start and end apart: 2 -> 2, of which waited for: 0 -> 1; matrix products, arithmetic and copies ran while one was open for 7% -> 5% of each run, Pallas kernels for 6% -> 4%
where the time goes in v5:
time: 62.5 us; the launch traced here: 62.2 us
  blocking collectives  28.6 us (46%)
  Pallas kernels  15.3 us (24%)
  starting transfers between devices  13.2 us (21%)
  other arithmetic  3.23 us (5%)
  waiting for transfers between devices  1.04 us (2%)
  between operations  0.77 us (1%)
    all_to_all x1, blocking collectives, per_device(): block = lax.all_to_all(message, ('slab', 'mode'), 0, 0, tiled=True)  16.4 us
    pallas_call x7, Pallas kernels, run(): pl.pallas_call(kernel, out_shape=outs, in_specs=_smem(smem) + _vmem(len(a...  15.3 us
    all_to_all x1, blocking collectives, per_device(): pieces = lax.all_to_all(result, ('slab', 'mode'), 0, 0, tiled=True)  12.2 us
    ppermute x1, starting transfers between devices, per_device(): lax.ppermute(to_left, 'pair', [(n + 1, n) for n in range(count - 1)])  8 us
    ppermute x1, starting transfers between devices, per_device(): lax.ppermute(to_right, 'pair', [(n, n + 1) for n in range(count - 1)])  5.18 us
    reduce_max x1, other arithmetic, pattern_tables(): high = jnp.max(jnp.where(match, code[:, None], -1), axis=0)  1.74 us
    reduce_sum x1, other arithmetic, pattern_tables(): jnp.sum(jnp.where(code[:, None] == high[None, :], coupling[:, None], 0.0)...  1.42 us
  transfers between devices with their start and end apart: 2, of which 1 were waited for; matrix products, arithmetic and copies ran while one was open for 5% of the time, Pallas kernels for 4%

profile of v5, /device:TPU:24, one launch (start us, length us, event | category | flops | bytes accessed | tf_op | source)
XLA Modules:
  0.0 62.2 jit_solution(5426546953080519302)
XLA Ops:
  0.6 0.0 copy-start
  0.6 1.5 %send.1 = f32[16,8,8,128]{3,2,1,0:T(8,128)S(1)} custom-call(s32[1]{0:T(128)} %bitcast.which_ref, f32[15,2,8,128]{3,2,1,0:T(8,128)} %guess_ref.1, f32[15,2,8,128]{3,2,1,0:T(8,128)} %source_ref.1, f32[2,8,128]{2,1,0:T(8,128)} %mean_ref.1, f32[7,2,8,128]{3,2,1,0:T(8,128)} %fluct_ref.1), custom_call_target="tpu_custom_call" | custom-call | tf_op jit(solution)/shard_map/send/pallas_call | solution.py:377
  2.2 0.0 copy-start.2
  2.2 16.4 %all_to_all.10.block_ref = f32[16,8,8,128]{3,2,1,0:T(8,128)S(1)} all-to-all(f32[16,8,8,128]{3,2,1,0:T(8,128)S(1)} %send.1), channel_id=1, replica_groups=mesh['pair'=32,'slab'=2,'mode'=8] {'slab','mode'}, dimensions={0} | all-to-all | bytes 1048576 | tf_op jit(solution)/shard_map/all_to_all | solution.py:406
  18.6 0.0 copy-done
  18.6 0.0 copy-start.3
  18.6 0.3 halo_right.1
  18.9 5.2 %collective-permute-start = (f32[8,2,3,8,128]{4,3,2,1,0:T(8,128)S(1)}, f32[8,2,3,8,128]{4,3,2,1,0:T(8,128)S(1)}, u32[]{:S(2)}, u32[]{:S(2)}) collective-permute-start(f32[8,2,3,8,128]{4,3,2,1,0:T(8,128)S(1)} %halo_right.1), channel_id=1, source_target_pairs={{0,16},{16,32},{32,48},{48,64},{64,80},{80,96},{96,112},{112,128},... | collective-permute-start | bytes 589832 | tf_op jit(solution)/shard_map/ppermute | solution.py:410
  24.1 0.0 copy-done.2
  24.1 0.1 slice_reduce_fusion
  24.2 0.3 halo_left.1
  24.5 0.0 copy-start.1
  24.5 8.0 %collective-permute-start.1 = (f32[8,2,3,8,128]{4,3,2,1,0:T(8,128)S(1)}, f32[8,2,3,8,128]{4,3,2,1,0:T(8,128)S(1)}, u32[]{:S(2)}, u32[]{:S(2)}) collective-permute-start(f32[8,2,3,8,128]{4,3,2,1,0:T(8,128)S(1)} %halo_left.1), channel_id=1, source_target_pairs={{16,0},{32,16},{48,32},{64,48},{80,64},{96,80},{112,96},{128,112},... | collective-permute-start | bytes 589832 | tf_op jit(solution)/shard_map/ppermute | solution.py:412
  32.5 1.7 %select_reduce_fusion.2 = (s32[840]{0:T(1024)S(1)}, s32[840]{0:T(1024)S(1)}) fusion(s32[1680]{0:T(1024)S(1)} %get-tuple-element.13, s32[1680]{0:T(1024)S(1)} %multiply_add_fusion), kind=kLoop, calls=%fused_computation.2 | loop fusion | flops 7054320 | bytes 20160 | tf_op jit(solution)/shard_map/reduce_max | solution.py:365
  34.3 0.0 copy-done.3
  34.3 1.4 %select_reduce_fusion = (f32[840]{0:T(1024)S(1)}, f32[840]{0:T(1024)S(1)}) fusion(s32[840]{0:T(1024)S(1)} %get-tuple-element.16, f32[1680]{0:T(1024)S(1)} %copy-done.3, s32[1680]{0:T(1024)S(1)} %multiply_add_fusion, s32[840]{0:T(1024)S(1)} %get-tuple-element.17), kind=kLoop, calls=%fused_computation | loop fusion | flops 8465520 | bytes 26880 | tf_op jit(solution)/shard_map/reduce_sum | solution.py:367
  35.7 2.0 %values.1.value_ref = f32[1680,128]{1,0:T(8,128)S(1)} custom-call(f32[840]{0:T(1024)S(1)} %get-tuple-element.15.c1_ref, f32[840]{0:T(1024)S(1)} %get-tuple-element.14.c2_ref), custom_call_target="tpu_custom_call" | custom-call | tf_op jit(solution)/shard_map/values/pallas_call | solution.py:377
  37.7 0.5 own.1
  38.2 1.0 %collective-permute-done.1.right_ref = f32[8,2,3,8,128]{4,3,2,1,0:T(8,128)S(1)} collective-permute-done((f32[8,2,3,8,128]{4,3,2,1,0:T(8,128)S(1)}, f32[8,2,3,8,128]{4,3,2,1,0:T(8,128)S(1)}, u32[]{:S(2)}, u32[]{:S(2)}) %collective-permute-start.1) | collective-permute-done | bytes 196640 | tf_op jit(solution)/shard_map/ppermute | solution.py:412
  39.3 0.0 collective-permute-done.left_ref
  39.3 0.0 copy-done.1
  39.3 9.6 %sweeps.1 = f32[16,4,8,128]{3,2,1,0:T(8,128)S(1)} custom-call(s32[840]{0:T(1024)S(1)} %get-tuple-element.19.j1_ref, s32[840]{0:T(1024)S(1)} %get-tuple-element.18.j2_ref, f32[1680,128]{1,0:T(8,128)S(1)} %values.1.value_ref, s32[32,128]{1,0:T(8,128)S(1)} %copy-done, bf16[384,128]{1,0:T(8,128)(2,1)S(1)} %copy-done.1, ...), custom_call_target="tpu_custom_call" | custom-call | tf_op jit(solution)/shard_map/sweeps/pallas_call | solution.py:377
  48.9 12.2 %all_to_all.11.piece_ref = f32[16,4,8,128]{3,2,1,0:T(8,128)S(1)} all-to-all(f32[16,4,8,128]{3,2,1,0:T(8,128)S(1)} %sweeps.1), channel_id=1, replica_groups=mesh['pair'=32,'slab'=2,'mode'=8] {'slab','mode'}, dimensions={0} | all-to-all | bytes 524288 | tf_op jit(solution)/shard_map/all_to_all | solution.py:425
  61.1 1.1 %receive.1 = (f32[15,2,8,128]{3,2,1,0:T(8,128)}, f32[15,2,8,128]{3,2,1,0:T(8,128)}) custom-call(f32[16,4,8,128]{3,2,1,0:T(8,128)S(1)} %all_to_all.11.piece_ref), custom_call_target="tpu_custom_call" | custom-call | tf_op jit(solution)/shard_map/receive/pallas_call | solution.py:377
  (2 shorter events, 0.0 us)
Async XLA Ops:
  0.6 18.0 %copy-start = (s32[32,128]{1,0:T(8,128)S(1)}, s32[32,128]{1,0:T(8,128)}, u32[]{:S(2)}) copy-start(s32[32,128]{1,0:T(8,128)} %constant.28.clone.table_ref) | copy-start | bytes 49156
  2.2 21.9 %copy-start.2 = (s32[3,1680]{1,0:T(4,128)S(1)}, s32[3,1680]{1,0:T(4,128)}, u32[]{:S(2)}) copy-start(s32[3,1680]{1,0:T(4,128)} %param.12) | copy-start | bytes 60484
  18.6 15.7 %copy-start.3 = (f32[1680]{0:T(1024)S(1)}, f32[1680]{0:T(1024)}, u32[]{:S(2)}) copy-start(f32[1680]{0:T(1024)} %param.13) | copy-start | bytes 20164
  18.9 20.4 %collective-permute-start = (f32[8,2,3,8,128]{4,3,2,1,0:T(8,128)S(1)}, f32[8,2,3,8,128]{4,3,2,1,0:T(8,128)S(1)}, u32[]{:S(2)}, u32[]{:S(2)}) collective-permute-start(f32[8,2,3,8,128]{4,3,2,1,0:T(8,128)S(1)} %halo_right.1), channel_id=1, source_target_pairs={{0,16},{16,32},{32,48},{48,64},{64,80},{80,96},{96,112},{112,128},... | collective-permute-start | bytes 589832 | tf_op jit(solution)/shard_map/ppermute | solution.py:410
  24.5 14.8 %copy-start.1 = (bf16[384,128]{1,0:T(8,128)(2,1)S(1)}, bf16[384,128]{1,0:T(8,128)(2,1)}, u32[]{:S(2)}) copy-start(bf16[384,128]{1,0:T(8,128)(2,1)} %constant.29.clone.near_ref) | copy-start | bytes 294916
  24.5 14.8 %collective-permute-start.1 = (f32[8,2,3,8,128]{4,3,2,1,0:T(8,128)S(1)}, f32[8,2,3,8,128]{4,3,2,1,0:T(8,128)S(1)}, u32[]{:S(2)}, u32[]{:S(2)}) collective-permute-start(f32[8,2,3,8,128]{4,3,2,1,0:T(8,128)S(1)} %halo_left.1), channel_id=1, source_target_pairs={{16,0},{32,16},{48,32},{64,48},{80,64},{96,80},{112,96},{128,112},... | collective-permute-start | bytes 589832 | tf_op jit(solution)/shard_map/ppermute | solution.py:412

commit v6 on v5

--- a/solution.py
+++ b/solution.py
@@ -332,8 +332,9 @@
                 out_ref[slab * PARTS + md, t] = tile
 
 
-def _receive_kernel(piece_ref, solution_ref, update_ref):
+def _receive_kernel(piece_ref, solution_ref, update_ref, kept_ref, sems):
     lane = _lane()
+    copies = []
     for t in range(4):
         rolled = [_roll(piece_ref[q, t], ZW * q) for q in range(GROUP)]
         for h in range(GROUP):
@@ -344,7 +345,13 @@
             tile = rolled[0]
             for q in range(1, GROUP):
                 tile = jnp.where(shifted >= ZW * q, rolled[q], tile)
-            (solution_ref, update_ref)[n // 2][m, n % 2] = _roll(tile, -ZW * h)
+            kept_ref[n // 2, m, n % 2] = _roll(tile, -ZW * h)
+        part = pl.ds(4 * t, min(4, BLOCK - 4 * t))
+        for n, out_ref in enumerate((solution_ref, update_ref)):
+            copies.append(pltpu.make_async_copy(kept_ref.at[n, part], out_ref.at[part], sems.at[2 * t + n]))
+            copies[-1].start()
+    for copy in copies:
+        copy.wait()
 
 
 def _vmem(count):
@@ -423,8 +430,17 @@
         j1, j2, values, table, near, *own, from_left, from_right
     )
     pieces = lax.all_to_all(result, ("slab", "mode"), 0, 0, tiled=True)
-    outs = [jax.ShapeDtypeStruct(guess.shape, F32)] * 2
-    return tuple(_call(_receive_kernel, outs, 0, "receive")(pieces))
+    return tuple(
+        pl.pallas_call(
+            _receive_kernel,
+            out_shape=[jax.ShapeDtypeStruct(guess.shape, F32)] * 2,
+            in_specs=_vmem(1),
+            out_specs=[pl.BlockSpec(memory_space=pl.ANY)] * 2,
+            scratch_shapes=[pltpu.VMEM((2,) + guess.shape, F32), pltpu.SemaphoreType.DMA((8,))],
+            compiler_params=pltpu.CompilerParams(vmem_limit_bytes=24 << 20),
+            name="receive",
+        )(pltpu.with_memory_space_constraint(pieces, pltpu.VMEM))
+    )
 
 
 def solution(mesh):

time: 62.5 us -> 62.5 us (level)
    pallas_call x0 -> x1, Pallas kernels: none -> 1.05 us  [per_device(): pl.pallas_call(_receive_kernel, out_shape=[jax.ShapeDtypeStruct(guess.sha...]
    pallas_call x7 -> x6, Pallas kernels: 15.3 us -> 14.3 us  [run(): pl.pallas_call(kernel, out_shape=outs, in_specs=_smem(smem) + _vmem(len(a...]
where the time goes in v6:
time: 62.5 us; the launch traced here: 62.2 us
  blocking collectives  28.6 us (46%)
  Pallas kernels  15.3 us (24%)
  starting transfers between devices  13.2 us (21%)
  other arithmetic  3.23 us (5%)
  waiting for transfers between devices  1.04 us (2%)
  between operations  0.77 us (1%)
    all_to_all x1, blocking collectives, per_device(): block = lax.all_to_all(message, ('slab', 'mode'), 0, 0, tiled=True)  16.4 us
    pallas_call x6, Pallas kernels, run(): pl.pallas_call(kernel, out_shape=outs, in_specs=_smem(smem) + _vmem(len(a...  14.3 us
    all_to_all x1, blocking collectives, per_device(): pieces = lax.all_to_all(result, ('slab', 'mode'), 0, 0, tiled=True)  12.2 us
    ppermute x1, starting transfers between devices, per_device(): lax.ppermute(to_left, 'pair', [(n + 1, n) for n in range(count - 1)])  8 us
    ppermute x1, starting transfers between devices, per_device(): lax.ppermute(to_right, 'pair', [(n, n + 1) for n in range(count - 1)])  5.18 us
    reduce_max x1, other arithmetic, pattern_tables(): high = jnp.max(jnp.where(match, code[:, None], -1), axis=0)  1.74 us
    reduce_sum x1, other arithmetic, pattern_tables(): jnp.sum(jnp.where(code[:, None] == high[None, :], coupling[:, None], 0.0)...  1.42 us
  transfers between devices with their start and end apart: 2, of which 1 were waited for; matrix products, arithmetic and copies ran while one was open for 5% of the time, Pallas kernels for 4%

profile of v6, /device:TPU:24, one launch (start us, length us, event | category | flops | bytes accessed | tf_op | source)
XLA Modules:
  0.0 62.2 jit_solution(3165534380613367036)
XLA Ops:
  0.6 0.0 copy-start
  0.6 1.5 %send.1 = f32[16,8,8,128]{3,2,1,0:T(8,128)S(1)} custom-call(s32[1]{0:T(128)} %bitcast.which_ref, f32[15,2,8,128]{3,2,1,0:T(8,128)} %guess_ref.1, f32[15,2,8,128]{3,2,1,0:T(8,128)} %source_ref.1, f32[2,8,128]{2,1,0:T(8,128)} %mean_ref.1, f32[7,2,8,128]{3,2,1,0:T(8,128)} %fluct_ref.1), custom_call_target="tpu_custom_call" | custom-call | tf_op jit(solution)/shard_map/send/pallas_call | solution.py:384
  2.2 0.0 copy-start.2
  2.2 16.4 %all_to_all.10.block_ref = f32[16,8,8,128]{3,2,1,0:T(8,128)S(1)} all-to-all(f32[16,8,8,128]{3,2,1,0:T(8,128)S(1)} %send.1), channel_id=1, replica_groups=mesh['pair'=32,'slab'=2,'mode'=8] {'slab','mode'}, dimensions={0} | all-to-all | bytes 1048576 | tf_op jit(solution)/shard_map/all_to_all | solution.py:413
  18.6 0.0 copy-done
  18.6 0.0 copy-start.3
  18.6 0.3 halo_right.1
  18.9 5.2 %collective-permute-start = (f32[8,2,3,8,128]{4,3,2,1,0:T(8,128)S(1)}, f32[8,2,3,8,128]{4,3,2,1,0:T(8,128)S(1)}, u32[]{:S(2)}, u32[]{:S(2)}) collective-permute-start(f32[8,2,3,8,128]{4,3,2,1,0:T(8,128)S(1)} %halo_right.1), channel_id=1, source_target_pairs={{0,16},{16,32},{32,48},{48,64},{64,80},{80,96},{96,112},{112,128},... | collective-permute-start | bytes 589832 | tf_op jit(solution)/shard_map/ppermute | solution.py:417
  24.1 0.0 copy-done.2
  24.1 0.1 slice_reduce_fusion
  24.2 0.3 halo_left.1
  24.5 0.0 copy-start.1
  24.5 8.0 %collective-permute-start.1 = (f32[8,2,3,8,128]{4,3,2,1,0:T(8,128)S(1)}, f32[8,2,3,8,128]{4,3,2,1,0:T(8,128)S(1)}, u32[]{:S(2)}, u32[]{:S(2)}) collective-permute-start(f32[8,2,3,8,128]{4,3,2,1,0:T(8,128)S(1)} %halo_left.1), channel_id=1, source_target_pairs={{16,0},{32,16},{48,32},{64,48},{80,64},{96,80},{112,96},{128,112},... | collective-permute-start | bytes 589832 | tf_op jit(solution)/shard_map/ppermute | solution.py:419
  32.5 1.7 %select_reduce_fusion.2 = (s32[840]{0:T(1024)S(1)}, s32[840]{0:T(1024)S(1)}) fusion(s32[1680]{0:T(1024)S(1)} %get-tuple-element.13, s32[1680]{0:T(1024)S(1)} %multiply_add_fusion), kind=kLoop, calls=%fused_computation.2 | loop fusion | flops 7054320 | bytes 20160 | tf_op jit(solution)/shard_map/reduce_max | solution.py:372
  34.3 0.0 copy-done.3
  34.3 1.4 %select_reduce_fusion = (f32[840]{0:T(1024)S(1)}, f32[840]{0:T(1024)S(1)}) fusion(s32[840]{0:T(1024)S(1)} %get-tuple-element.16, f32[1680]{0:T(1024)S(1)} %copy-done.3, s32[1680]{0:T(1024)S(1)} %multiply_add_fusion, s32[840]{0:T(1024)S(1)} %get-tuple-element.17), kind=kLoop, calls=%fused_computation | loop fusion | flops 8465520 | bytes 26880 | tf_op jit(solution)/shard_map/reduce_sum | solution.py:374
  35.7 2.0 %values.1.value_ref = f32[1680,128]{1,0:T(8,128)S(1)} custom-call(f32[840]{0:T(1024)S(1)} %get-tuple-element.15.c1_ref, f32[840]{0:T(1024)S(1)} %get-tuple-element.14.c2_ref), custom_call_target="tpu_custom_call" | custom-call | tf_op jit(solution)/shard_map/values/pallas_call | solution.py:384
  37.7 0.5 own.1
  38.2 1.0 %collective-permute-done.1.right_ref = f32[8,2,3,8,128]{4,3,2,1,0:T(8,128)S(1)} collective-permute-done((f32[8,2,3,8,128]{4,3,2,1,0:T(8,128)S(1)}, f32[8,2,3,8,128]{4,3,2,1,0:T(8,128)S(1)}, u32[]{:S(2)}, u32[]{:S(2)}) %collective-permute-start.1) | collective-permute-done | bytes 196640 | tf_op jit(solution)/shard_map/ppermute | solution.py:419
  39.3 0.0 collective-permute-done.left_ref
  39.3 0.0 copy-done.1
  39.3 9.6 %sweeps.1 = f32[16,4,8,128]{3,2,1,0:T(8,128)S(1)} custom-call(s32[840]{0:T(1024)S(1)} %get-tuple-element.19.j1_ref, s32[840]{0:T(1024)S(1)} %get-tuple-element.18.j2_ref, f32[1680,128]{1,0:T(8,128)S(1)} %values.1.value_ref, s32[32,128]{1,0:T(8,128)S(1)} %copy-done, bf16[384,128]{1,0:T(8,128)(2,1)S(1)} %copy-done.1, ...), custom_call_target="tpu_custom_call" | custom-call | tf_op jit(solution)/shard_map/sweeps/pallas_call | solution.py:384
  48.9 12.2 %all_to_all.11.piece_ref = f32[16,4,8,128]{3,2,1,0:T(8,128)S(1)} all-to-all(f32[16,4,8,128]{3,2,1,0:T(8,128)S(1)} %sweeps.1), channel_id=1, replica_groups=mesh['pair'=32,'slab'=2,'mode'=8] {'slab','mode'}, dimensions={0} | all-to-all | bytes 524288 | tf_op jit(solution)/shard_map/all_to_all | solution.py:432
  61.1 1.1 %receive.1 = (f32[15,2,8,128]{3,2,1,0:T(8,128)}, f32[15,2,8,128]{3,2,1,0:T(8,128)}) custom-call(f32[16,4,8,128]{3,2,1,0:T(8,128)S(1)} %all_to_all.11.piece_ref), custom_call_target="tpu_custom_call" | custom-call | tf_op jit(solution)/shard_map/receive/pallas_call | solution.py:434
  (2 shorter events, 0.0 us)
Async XLA Ops:
  0.6 18.0 %copy-start = (s32[32,128]{1,0:T(8,128)S(1)}, s32[32,128]{1,0:T(8,128)}, u32[]{:S(2)}) copy-start(s32[32,128]{1,0:T(8,128)} %constant.28.clone.table_ref) | copy-start | bytes 49156
  2.2 21.9 %copy-start.2 = (s32[3,1680]{1,0:T(4,128)S(1)}, s32[3,1680]{1,0:T(4,128)}, u32[]{:S(2)}) copy-start(s32[3,1680]{1,0:T(4,128)} %param.12) | copy-start | bytes 60484
  18.6 15.7 %copy-start.3 = (f32[1680]{0:T(1024)S(1)}, f32[1680]{0:T(1024)}, u32[]{:S(2)}) copy-start(f32[1680]{0:T(1024)} %param.13) | copy-start | bytes 20164
  18.9 20.4 %collective-permute-start = (f32[8,2,3,8,128]{4,3,2,1,0:T(8,128)S(1)}, f32[8,2,3,8,128]{4,3,2,1,0:T(8,128)S(1)}, u32[]{:S(2)}, u32[]{:S(2)}) collective-permute-start(f32[8,2,3,8,128]{4,3,2,1,0:T(8,128)S(1)} %halo_right.1), channel_id=1, source_target_pairs={{0,16},{16,32},{32,48},{48,64},{64,80},{80,96},{96,112},{112,128},... | collective-permute-start | bytes 589832 | tf_op jit(solution)/shard_map/ppermute | solution.py:417
  24.5 14.8 %copy-start.1 = (bf16[384,128]{1,0:T(8,128)(2,1)S(1)}, bf16[384,128]{1,0:T(8,128)(2,1)}, u32[]{:S(2)}) copy-start(bf16[384,128]{1,0:T(8,128)(2,1)} %constant.29.clone.near_ref) | copy-start | bytes 294916
  24.5 14.8 %collective-permute-start.1 = (f32[8,2,3,8,128]{4,3,2,1,0:T(8,128)S(1)}, f32[8,2,3,8,128]{4,3,2,1,0:T(8,128)S(1)}, u32[]{:S(2)}, u32[]{:S(2)}) collective-permute-start(f32[8,2,3,8,128]{4,3,2,1,0:T(8,128)S(1)} %halo_left.1), channel_id=1, source_target_pairs={{16,0},{32,16},{48,32},{64,48},{80,64},{96,80},{112,96},{128,112},... | collective-permute-start | bytes 589832 | tf_op jit(solution)/shard_map/ppermute | solution.py:419
